TPU v7x, 128 devices: a whole 4x4x4 slice. The times are simulated.
128 devices in a mesh: dp: 4 (over z_lo, core), ctx: 32 (over z_hi, x, y).
Axes of the slice: x: 4, y: 4, z: 4 (z_hi: 2, z_lo: 2; z = z_hi * 2 + z_lo), core: 2. Of those that a mesh axis runs over, the one named last changes fastest.
Arguments:
- queries: bfloat16 [4, 4096, 4096], P('dp', 'ctx'), may hold values from -256 to 256
- keys: bfloat16 [4, 4096, 4096], P('dp', 'ctx'), may hold values from -4 to 4
- gate: bfloat16 [4, 4096, 4096], P('dp', 'ctx'), may hold values from -6 to 6
- values: bfloat16 [4, 4096, 4096], P('dp', 'ctx'), may hold values from -6 to 6
- grad_out: bfloat16 [4, 4096, 4096], P('dp', 'ctx'), may hold values from -3 to 3
- doc_start: int32 [4, 4096], P('dp', 'ctx'), may hold values from 0 to 4095, as said below
- filter_taps: float32 [128, 4096], replicated, may hold values from -0.5 to 0.5
Outputs:
- grad_queries: bfloat16 [4, 4096, 4096], P('dp', 'ctx')
- grad_keys: bfloat16 [4, 4096, 4096], P('dp', 'ctx')
- grad_gate: bfloat16 [4, 4096, 4096], P('dp', 'ctx')
- grad_values: bfloat16 [4, 4096, 4096], P('dp', 'ctx')
- grad_filter: float32 [128, 4096], replicated
Inputs may be any that keep to these rules, and one draw needn't show every extreme that they name: `doc_start`: entry t of a sequence is the first position of the document that holds position t: it never exceeds t and never falls along the sequence; every document has at most 640 positions, and every sequence holds one of exactly 640 positions.
All inputs are finite; a program needn't handle non-finite values.
Results may differ from a plain program's by a relative error of at most 0.0087.
Values may be sent and summed in bfloat16 or wider, within the bound.
No kernel may reach another device: no remote copies, remote signals or barrier semaphores. Data moves between devices by JAX's collectives and lax.ppermute only.
A program may use at most 192 MiB of HBM per device.

v0:
```python
import jax
import jax.numpy as jnp
from jax import lax
from jax.sharding import PartitionSpec as P

HEADS = 32
ATT_HOPS = 5


lowest_score = -1e30


def passed_along(x, axis, by):
    length = lax.axis_size(axis)
    pairs = [(i, i + by) for i in range(length) if 0 <= i + by < length]
    return lax.ppermute(x, axis, pairs)


def on_device(queries, keys, gate, values, grad_out, doc_start, filter_taps):
    highest = lax.Precision.HIGHEST
    tok_rows = queries.shape[1]
    channel_count = queries.shape[2]
    tap_count = filter_taps.shape[0]
    tap_group = 16
    group_count = tap_count // tap_group
    rim_len = tap_count - 1
    head_width = channel_count // HEADS
    score_scale = head_width ** (-0.5)
    device_rank = lax.axis_index("ctx")
    stream_len = lax.axis_size("ctx") * tok_rows
    own_first = device_rank * tok_rows
    own_pos = own_first + jnp.arange(tok_rows, dtype=jnp.int32)
    own_start = doc_start[0]
    local_values = values[0]
    distance = 1
    first_row = max(0, distance * tok_rows - rim_len)
    behind = [passed_along(local_values[first_row:], "ctx", distance)]
    extended = jnp.concatenate(behind + [local_values], 0).astype(jnp.float32)

    def add_group(group_index, summed):
        base = group_index * tap_group
        block_taps = lax.dynamic_slice_in_dim(filter_taps, base, tap_group, 0)
        region = lax.dynamic_slice_in_dim(
            extended, rim_len - base - (tap_group - 1), tok_rows + tap_group - 1, 0
        )
        for inner in range(tap_group):
            lead = tap_group - 1 - inner
            summed = summed + block_taps[inner][None, :] * region[lead : lead + tok_rows]
        return summed

    mixed = lax.fori_loop(
        0, group_count, add_group, jnp.zeros((tok_rows, channel_count), jnp.float32)
    )
    gate_f32 = gate[0].astype(jnp.float32)
    hyena_out = (gate_f32 * mixed).astype(jnp.bfloat16)
    query_heads = queries[0].reshape(tok_rows, HEADS, head_width)
    key_heads = keys[0].reshape(tok_rows, HEADS, head_width)
    grad_heads = grad_out[0].reshape(tok_rows, HEADS, head_width)
    hyena_heads = hyena_out.reshape(tok_rows, HEADS, head_width)
    grad_f32 = grad_heads.astype(jnp.float32)

    def scores_of(key_piece, offset):
        piece_rows = key_piece.shape[0]
        key_split = key_piece.reshape(piece_rows, HEADS, head_width)
        key_pos = offset + jnp.arange(piece_rows, dtype=jnp.int32)
        allowed = (key_pos[None, :] <= own_pos[:, None]) & (key_pos[None, :] >= own_start[:, None])
        scores = (
            jnp.einsum("ihe,jhe->hij", query_heads, key_split, preferred_element_type=jnp.float32)
            * score_scale
        )
        return (key_split, allowed, scores)

    blocks = [(keys[0], hyena_out, own_first)]
    for distance in range(1, ATT_HOPS + 1):
        key_piece, value_piece = passed_along((keys[0], hyena_out), "ctx", distance)
        blocks.append((key_piece, value_piece, own_first - distance * tok_rows))
    row_top = jnp.full((HEADS, tok_rows), lowest_score, jnp.float32)
    totals = jnp.zeros((HEADS, tok_rows), jnp.float32)
    for key_piece, value_piece, offset in blocks:
        key_split, allowed, scores = scores_of(key_piece, offset)
        new_top = jnp.maximum(row_top, jnp.max(jnp.where(allowed[None], scores, lowest_score), -1))
        weights = jnp.where(allowed[None], jnp.exp(scores - new_top[:, :, None]), 0.0)
        totals = totals * jnp.exp(row_top - new_top) + jnp.sum(weights, -1)
        row_top = new_top
    log_sums = row_top + jnp.log(totals)
    attended = jnp.zeros((tok_rows, HEADS, head_width), jnp.float32)
    for key_piece, value_piece, offset in blocks:
        key_split, allowed, scores = scores_of(key_piece, offset)
        value_split = value_piece.reshape(value_piece.shape[0], HEADS, head_width)
        probs_half = jnp.where(allowed[None], jnp.exp(scores - log_sums[:, :, None]), 0.0).astype(
            jnp.bfloat16
        )
        attended = attended + jnp.einsum(
            "hij,jhe->ihe", probs_half, value_split, preferred_element_type=jnp.float32
        )
    deltas = jnp.einsum("ihe,ihe->hi", grad_f32, attended, precision=highest)
    query_acc = jnp.zeros((tok_rows, HEADS, head_width), jnp.float32)
    for block_index in range(len(blocks)):
        key_piece, value_piece, offset = blocks[block_index]
        key_split, allowed, scores = scores_of(key_piece, offset)
        value_split = value_piece.reshape(value_piece.shape[0], HEADS, head_width)
        probs = jnp.where(allowed[None], jnp.exp(scores - log_sums[:, :, None]), 0.0)
        dprob = jnp.einsum(
            "ihe,jhe->hij", grad_heads, value_split, preferred_element_type=jnp.float32
        )
        dscore = (probs * (dprob - deltas[:, :, None])).astype(jnp.bfloat16)
        query_acc = query_acc + jnp.einsum(
            "hij,jhe->ihe", dscore, key_split, preferred_element_type=jnp.float32
        )
    grad_query = (query_acc * score_scale).reshape(tok_rows, channel_count).astype(jnp.bfloat16)
    own_pos_f32 = own_pos.astype(jnp.float32)
    start_f32 = own_start.astype(jnp.float32)[None, :]

    def query_step(acc_pair, pieces, stats, offset):
        query_piece, grad_piece = pieces
        log_piece, delta_piece, start_piece = stats
        piece_rows = query_piece.shape[0]
        query_piece = query_piece.reshape(piece_rows, HEADS, head_width)
        grad_piece = grad_piece.reshape(piece_rows, HEADS, head_width)
        query_pos = offset + jnp.arange(piece_rows, dtype=jnp.int32)
        start_row = start_piece[0]
        allowed = (own_pos[None, :] <= query_pos[:, None]) & (
            own_pos_f32[None, :] >= start_row[:, None]
        )
        allowed = allowed & (query_pos[:, None] < stream_len)
        scores = (
            jnp.einsum("ihe,jhe->hij", query_piece, key_heads, preferred_element_type=jnp.float32)
            * score_scale
        )
        probs = jnp.where(allowed[None], jnp.exp(scores - log_piece[:, :, None]), 0.0)
        probs_half = probs.astype(jnp.bfloat16)
        dprob = jnp.einsum(
            "ihe,jhe->hij", grad_piece, hyena_heads, preferred_element_type=jnp.float32
        )
        dscore = (probs * (dprob - delta_piece[:, :, None])).astype(jnp.bfloat16)
        acc_dkey, acc_dvalue = acc_pair
        acc_dkey = acc_dkey + jnp.einsum(
            "hij,ihe->jhe", dscore, query_piece, preferred_element_type=jnp.float32
        )
        acc_dvalue = acc_dvalue + jnp.einsum(
            "hij,ihe->jhe", probs_half, grad_piece, preferred_element_type=jnp.float32
        )
        return (acc_dkey, acc_dvalue)

    head_zeros = jnp.zeros((tok_rows, HEADS, head_width), jnp.float32)
    acc_pair = query_step(
        (head_zeros, head_zeros),
        (queries[0], grad_out[0]),
        (log_sums, deltas, start_f32),
        own_first,
    )
    for distance in range(1, ATT_HOPS + 1):
        query_piece, grad_piece = passed_along((queries[0], grad_out[0]), "ctx", -distance)
        stats = passed_along((log_sums, deltas, start_f32), "ctx", -distance)
        acc_pair = query_step(
            acc_pair, (query_piece, grad_piece), stats, own_first + distance * tok_rows
        )
    key_grad = (acc_pair[0] * score_scale).reshape(tok_rows, channel_count)
    value_grad = acc_pair[1].reshape(tok_rows, channel_count)
    grad_key = key_grad.astype(jnp.bfloat16)
    grad_gate = (value_grad * mixed).astype(jnp.bfloat16)
    grad_mixed = (value_grad * gate_f32).astype(jnp.bfloat16)
    distance = 1
    end_row = min(tok_rows, rim_len - (distance - 1) * tok_rows)
    ahead = [passed_along(grad_mixed[:end_row], "ctx", -distance)]
    grad_extended = jnp.concatenate([grad_mixed] + ahead, 0).astype(jnp.float32)

    def back_group(group_index, summed):
        base = group_index * tap_group
        block_taps = lax.dynamic_slice_in_dim(filter_taps, base, tap_group, 0)
        region = lax.dynamic_slice_in_dim(grad_extended, base, tok_rows + tap_group - 1, 0)
        for inner in range(tap_group):
            summed = summed + block_taps[inner][None, :] * region[inner : inner + tok_rows]
        return summed

    grad_values = lax.fori_loop(
        0, group_count, back_group, jnp.zeros((tok_rows, channel_count), jnp.float32)
    )
    grad_local = grad_mixed.astype(jnp.float32)

    def group_sums(group_index):
        base = group_index * tap_group
        region = lax.dynamic_slice_in_dim(
            extended, rim_len - base - (tap_group - 1), tok_rows + tap_group - 1, 0
        )
        rows_out = []
        for inner in range(tap_group):
            lead = tap_group - 1 - inner
            rows_out.append(jnp.sum(grad_local * region[lead : lead + tok_rows], 0))
        return jnp.stack(rows_out, 0)

    filter_terms = lax.map(group_sums, jnp.arange(group_count, dtype=jnp.int32)).reshape(
        tap_count, channel_count
    )
    grad_filter = lax.psum(filter_terms, ("dp", "ctx"))
    return (
        grad_query[None],
        grad_key[None],
        grad_gate[None],
        grad_values.astype(jnp.bfloat16)[None],
        grad_filter,
    )


def solution(mesh):
    placed = (
        P("dp", "ctx", None),
        P("dp", "ctx", None),
        P("dp", "ctx", None),
        P("dp", "ctx", None),
        P("dp", "ctx", None),
        P("dp", "ctx"),
        P(),
    )
    return jax.shard_map(
        on_device,
        mesh=mesh,
        in_specs=placed,
        out_specs=(
            P("dp", "ctx", None),
            P("dp", "ctx", None),
            P("dp", "ctx", None),
            P("dp", "ctx", None),
            P(),
        ),
        check_vma=False,
    )
```

profile of v0, /device:TPU:100, one launch (start us, length us, event | category | flops | bytes accessed | tf_op | source)
XLA Modules:
  0.0 1051.4 jit_solution(2082508625806646723)
XLA Ops:
  53.2 24.2 %collective-permute-done.5 = bf16[127,4096]{1,0:T(8,128)(2,1)} collective-permute-done((bf16[127,4096]{1,0:T(8,128)(2,1)}, bf16[127,4096]{1,0:T(8,128)(2,1)}, u32[]{:S(2)}, u32[]{:S(2)}) %collective-permute-start.5) | collective-permute-done | bytes 1040416 | tf_op jit(solution)/shard_map/ppermute | solution.py:16
  84.0 172.1 %while.47 = (s32[]{:T(128)}, f32[128,4096]{1,0:T(8,128)}, f32[128,4096]{1,0:T(8,128)}, f32[255,4096]{1,0:T(8,128)}, s32[]{:T(128)}, /*index=5*/s32[]{:T(128)}, s...) while((s32[]{:T(128)}, f32[128,4096]{1,0:T(8,128)}, ...), condition=%wide.region_13.14_spmd.clone, body=%wide.region_12.13_spmd.clone.sunk | while | flops 17301544 | bytes 38535976 | solution.py:51
  86.4 17.9 %fusion.401 = f32[128,4096]{1,0:T(8,128)} fusion(f32[255,4096]{1,0:T(8,128)} %get-tuple-element.727, s32[]{:T(128)S(6)} %select_n.270, s32[]{:T(128)S(6)} %add.1250, s32[]{:T(128)S(6)} %add.1251, s32[]{:T(128)S(6)} %add.1252, s32[]{:T(128)S(6)} %add.1253, s32[]{:T(128)S(6)} %add.1254, s32[]{:T(128)S(6)} %add.1255, s32[]{:T(128)S(6)} %add.1256, ...), kind=kLoop, calls=%fused_computation.34.clone.1 | loop fusion | flops 17301504 | bytes 38010944 | tf_op jit(solution)/shard_map/while/body/eval_jaxpr/add | solution.py:48
  106.8 18.7 %fusion.401 = f32[128,4096]{1,0:T(8,128)} fusion(f32[255,4096]{1,0:T(8,128)} %get-tuple-element.727, s32[]{:T(128)S(6)} %select_n.270, s32[]{:T(128)S(6)} %add.1250, s32[]{:T(128)S(6)} %add.1251, s32[]{:T(128)S(6)} %add.1252, s32[]{:T(128)S(6)} %add.1253, s32[]{:T(128)S(6)} %add.1254, s32[]{:T(128)S(6)} %add.1255, s32[]{:T(128)S(6)} %add.1256, ...), kind=kLoop, calls=%fused_computation.34.clone.1 | loop fusion | flops 17301504 | bytes 38010944 | tf_op jit(solution)/shard_map/while/body/eval_jaxpr/add | solution.py:48
  127.9 19.0 %fusion.401 = f32[128,4096]{1,0:T(8,128)} fusion(f32[255,4096]{1,0:T(8,128)} %get-tuple-element.727, s32[]{:T(128)S(6)} %select_n.270, s32[]{:T(128)S(6)} %add.1250, s32[]{:T(128)S(6)} %add.1251, s32[]{:T(128)S(6)} %add.1252, s32[]{:T(128)S(6)} %add.1253, s32[]{:T(128)S(6)} %add.1254, s32[]{:T(128)S(6)} %add.1255, s32[]{:T(128)S(6)} %add.1256, ...), kind=kLoop, calls=%fused_computation.34.clone.1 | loop fusion | flops 17301504 | bytes 38010944 | tf_op jit(solution)/shard_map/while/body/eval_jaxpr/add | solution.py:48
  149.3 19.5 %fusion.401 = f32[128,4096]{1,0:T(8,128)} fusion(f32[255,4096]{1,0:T(8,128)} %get-tuple-element.727, s32[]{:T(128)S(6)} %select_n.270, s32[]{:T(128)S(6)} %add.1250, s32[]{:T(128)S(6)} %add.1251, s32[]{:T(128)S(6)} %add.1252, s32[]{:T(128)S(6)} %add.1253, s32[]{:T(128)S(6)} %add.1254, s32[]{:T(128)S(6)} %add.1255, s32[]{:T(128)S(6)} %add.1256, ...), kind=kLoop, calls=%fused_computation.34.clone.1 | loop fusion | flops 17301504 | bytes 38010944 | tf_op jit(solution)/shard_map/while/body/eval_jaxpr/add | solution.py:48
  171.5 18.3 %fusion.401 = f32[128,4096]{1,0:T(8,128)} fusion(f32[255,4096]{1,0:T(8,128)} %get-tuple-element.727, s32[]{:T(128)S(6)} %select_n.270, s32[]{:T(128)S(6)} %add.1250, s32[]{:T(128)S(6)} %add.1251, s32[]{:T(128)S(6)} %add.1252, s32[]{:T(128)S(6)} %add.1253, s32[]{:T(128)S(6)} %add.1254, s32[]{:T(128)S(6)} %add.1255, s32[]{:T(128)S(6)} %add.1256, ...), kind=kLoop, calls=%fused_computation.34.clone.1 | loop fusion | flops 17301504 | bytes 38010944 | tf_op jit(solution)/shard_map/while/body/eval_jaxpr/add | solution.py:48
  192.3 18.8 %fusion.401 = f32[128,4096]{1,0:T(8,128)} fusion(f32[255,4096]{1,0:T(8,128)} %get-tuple-element.727, s32[]{:T(128)S(6)} %select_n.270, s32[]{:T(128)S(6)} %add.1250, s32[]{:T(128)S(6)} %add.1251, s32[]{:T(128)S(6)} %add.1252, s32[]{:T(128)S(6)} %add.1253, s32[]{:T(128)S(6)} %add.1254, s32[]{:T(128)S(6)} %add.1255, s32[]{:T(128)S(6)} %add.1256, ...), kind=kLoop, calls=%fused_computation.34.clone.1 | loop fusion | flops 17301504 | bytes 38010944 | tf_op jit(solution)/shard_map/while/body/eval_jaxpr/add | solution.py:48
  213.6 20.2 %fusion.401 = f32[128,4096]{1,0:T(8,128)} fusion(f32[255,4096]{1,0:T(8,128)} %get-tuple-element.727, s32[]{:T(128)S(6)} %select_n.270, s32[]{:T(128)S(6)} %add.1250, s32[]{:T(128)S(6)} %add.1251, s32[]{:T(128)S(6)} %add.1252, s32[]{:T(128)S(6)} %add.1253, s32[]{:T(128)S(6)} %add.1254, s32[]{:T(128)S(6)} %add.1255, s32[]{:T(128)S(6)} %add.1256, ...), kind=kLoop, calls=%fused_computation.34.clone.1 | loop fusion | flops 17301504 | bytes 38010944 | tf_op jit(solution)/shard_map/while/body/eval_jaxpr/add | solution.py:48
  236.0 20.1 %fusion.401 = f32[128,4096]{1,0:T(8,128)} fusion(f32[255,4096]{1,0:T(8,128)} %get-tuple-element.727, s32[]{:T(128)S(6)} %select_n.270, s32[]{:T(128)S(6)} %add.1250, s32[]{:T(128)S(6)} %add.1251, s32[]{:T(128)S(6)} %add.1252, s32[]{:T(128)S(6)} %add.1253, s32[]{:T(128)S(6)} %add.1254, s32[]{:T(128)S(6)} %add.1255, s32[]{:T(128)S(6)} %add.1256, ...), kind=kLoop, calls=%fused_computation.34.clone.1 | loop fusion | flops 17301504 | bytes 38010944 | tf_op jit(solution)/shard_map/while/body/eval_jaxpr/add | solution.py:48
  260.6 5.0 collective-permute-start.17
  267.5 12.5 %collective-permute-start.24 = (bf16[128,4096]{1,0:T(8,128)(2,1)}, bf16[128,4096]{1,0:T(8,128)(2,1)S(1)}, u32[]{:S(2)}, u32[]{:S(2)}) collective-permute-start(bf16[128,4096]{1,0:T(8,128)(2,1)} %bitcast.44), channel_id=1, source_target_pairs={{3,0},{4,1},{5,2},{6,3},{7,4},{8,5},{9,6},{10,7},{11,8},{12,9},{13... | collective-permute-start | bytes 3145736 | tf_op jit(solution)/shard_map/ppermute | solution.py:16
  286.1 9.6 collective-permute-start.12
  305.2 17.2 %collective-permute-done.17 = bf16[128,4096]{0,1:T(8,128)(2,1)S(1)} collective-permute-done((bf16[128,4096]{0,1:T(8,128)(2,1)S(1)}, bf16[128,4096]{0,1:T(8,128)(2,1)S(1)}, u32[]{:S(2)}, u32[]{:S(2)}) %collective-permute-start.17) | collective-permute-done | bytes 1048608 | tf_op jit(solution)/shard_map/ppermute | solution.py:16
  326.5 47.1 %collective-permute-done.12 = bf16[128,4096]{0,1:T(8,128)(2,1)S(1)} collective-permute-done((bf16[128,4096]{0,1:T(8,128)(2,1)S(1)}, bf16[128,4096]{0,1:T(8,128)(2,1)S(1)}, u32[]{:S(2)}, u32[]{:S(2)}) %collective-permute-start.12) | collective-permute-done | bytes 1048608 | tf_op jit(solution)/shard_map/ppermute | solution.py:16
  373.5 7.4 collective-permute-start.32
  383.6 46.7 %collective-permute-start.29 = (bf16[128,4096]{1,0:T(8,128)(2,1)}, bf16[128,4096]{1,0:T(8,128)(2,1)}, u32[]{:S(2)}, u32[]{:S(2)}) collective-permute-start(bf16[128,4096]{1,0:T(8,128)(2,1)} %bitcast.44), channel_id=1, source_target_pairs={{4,0},{5,1},{6,2},{7,3},{8,4},{9,5},{10,6},{11,7},{12,8},{13,9},{1... | collective-permute-start | bytes 3145736 | tf_op jit(solution)/shard_map/ppermute | solution.py:16
  437.2 25.7 %collective-permute-start.23 = (f32[32,128]{1,0:T(8,128)S(1)}, f32[32,128]{1,0:T(8,128)S(1)}, u32[]{:S(2)}, u32[]{:S(2)}) collective-permute-start(f32[32,128]{1,0:T(8,128)S(1)} %log_add_fusion), channel_id=1, source_target_pairs={{3,0},{4,1},{5,2},{6,3},{7,4},{8,5},{9,6},{10,7},{11,8},{12,9},{13... | collective-permute-start | bytes 49160 | tf_op jit(solution)/shard_map/ppermute | solution.py:16
  471.3 6.2 collective-permute-start.13
  479.8 9.8 collective-permute-start.28
  491.9 30.8 %collective-permute-start.33 = (f32[32,128]{1,0:T(8,128)S(1)}, f32[32,128]{1,0:T(8,128)S(1)}, u32[]{:S(2)}, u32[]{:S(2)}) collective-permute-start(f32[32,128]{1,0:T(8,128)S(1)} %log_add_fusion), channel_id=1, source_target_pairs={{5,0},{6,1},{7,2},{8,3},{9,4},{10,5},{11,6},{12,7},{13,8},{14,9},{... | collective-permute-start | bytes 49160 | tf_op jit(solution)/shard_map/ppermute | solution.py:16
  539.4 5.4 fusion.332
  554.5 5.7 collective-permute-start.36
  560.7 187.7 %while.46 = (s32[]{:T(128)}, f32[8,16,4096]{2,1,0:T(8,128)}, s32[8]{0:T(128)}, f32[255,4096]{1,0:T(8,128)}, f32[128,4096]{1,0:T(8,128)}, /*index=5*/s32[]{:T(128...) while((s32[]{:T(128)}, f32[8,16,4096]{2,1,0:T(8,128)}, ...), condition=%wide.region_33.34_spmd, body=%wide.region_16.33_spmd.sunk | while | flops 16711702 | bytes 36963352 | solution.py:192
  562.6 19.4 %fusion.400 = (f32[4096]{0:T(1024)S(1)}, f32[4096]{0:T(1024)S(1)}, f32[4096]{0:T(1024)S(1)}, f32[4096]{0:T(1024)S(1)}, f32[4096]{0:T(1024)S(1)}, /*index=5*/f32[...) fusion(f32[128,4096]{1,0:T(8,128)} %get-tuple-element.875, ...), kind=kLoop, calls=%fused_computation.1.clone.1 | loop fusion | flops 16711680 | bytes 35913792 | tf_op jit(solution)/shard_map/while/body/eval_jaxpr/reduce_sum | solution.py:189
  585.9 19.5 %fusion.400 = (f32[4096]{0:T(1024)S(1)}, f32[4096]{0:T(1024)S(1)}, f32[4096]{0:T(1024)S(1)}, f32[4096]{0:T(1024)S(1)}, f32[4096]{0:T(1024)S(1)}, /*index=5*/f32[...) fusion(f32[128,4096]{1,0:T(8,128)} %get-tuple-element.875, ...), kind=kLoop, calls=%fused_computation.1.clone.1 | loop fusion | flops 16711680 | bytes 35913792 | tf_op jit(solution)/shard_map/while/body/eval_jaxpr/reduce_sum | solution.py:189
  609.2 20.3 %fusion.400 = (f32[4096]{0:T(1024)S(1)}, f32[4096]{0:T(1024)S(1)}, f32[4096]{0:T(1024)S(1)}, f32[4096]{0:T(1024)S(1)}, f32[4096]{0:T(1024)S(1)}, /*index=5*/f32[...) fusion(f32[128,4096]{1,0:T(8,128)} %get-tuple-element.875, ...), kind=kLoop, calls=%fused_computation.1.clone.1 | loop fusion | flops 16711680 | bytes 35913792 | tf_op jit(solution)/shard_map/while/body/eval_jaxpr/reduce_sum | solution.py:189
  633.4 19.7 %fusion.400 = (f32[4096]{0:T(1024)S(1)}, f32[4096]{0:T(1024)S(1)}, f32[4096]{0:T(1024)S(1)}, f32[4096]{0:T(1024)S(1)}, f32[4096]{0:T(1024)S(1)}, /*index=5*/f32[...) fusion(f32[128,4096]{1,0:T(8,128)} %get-tuple-element.875, ...), kind=kLoop, calls=%fused_computation.1.clone.1 | loop fusion | flops 16711680 | bytes 35913792 | tf_op jit(solution)/shard_map/while/body/eval_jaxpr/reduce_sum | solution.py:189
  657.0 18.8 %fusion.400 = (f32[4096]{0:T(1024)S(1)}, f32[4096]{0:T(1024)S(1)}, f32[4096]{0:T(1024)S(1)}, f32[4096]{0:T(1024)S(1)}, f32[4096]{0:T(1024)S(1)}, /*index=5*/f32[...) fusion(f32[128,4096]{1,0:T(8,128)} %get-tuple-element.875, ...), kind=kLoop, calls=%fused_computation.1.clone.1 | loop fusion | flops 16711680 | bytes 35913792 | tf_op jit(solution)/shard_map/while/body/eval_jaxpr/reduce_sum | solution.py:189
  679.6 19.1 %fusion.400 = (f32[4096]{0:T(1024)S(1)}, f32[4096]{0:T(1024)S(1)}, f32[4096]{0:T(1024)S(1)}, f32[4096]{0:T(1024)S(1)}, f32[4096]{0:T(1024)S(1)}, /*index=5*/f32[...) fusion(f32[128,4096]{1,0:T(8,128)} %get-tuple-element.875, ...), kind=kLoop, calls=%fused_computation.1.clone.1 | loop fusion | flops 16711680 | bytes 35913792 | tf_op jit(solution)/shard_map/while/body/eval_jaxpr/reduce_sum | solution.py:189
  702.6 20.5 %fusion.400 = (f32[4096]{0:T(1024)S(1)}, f32[4096]{0:T(1024)S(1)}, f32[4096]{0:T(1024)S(1)}, f32[4096]{0:T(1024)S(1)}, f32[4096]{0:T(1024)S(1)}, /*index=5*/f32[...) fusion(f32[128,4096]{1,0:T(8,128)} %get-tuple-element.875, ...), kind=kLoop, calls=%fused_computation.1.clone.1 | loop fusion | flops 16711680 | bytes 35913792 | tf_op jit(solution)/shard_map/while/body/eval_jaxpr/reduce_sum | solution.py:189
  726.9 19.6 %fusion.400 = (f32[4096]{0:T(1024)S(1)}, f32[4096]{0:T(1024)S(1)}, f32[4096]{0:T(1024)S(1)}, f32[4096]{0:T(1024)S(1)}, f32[4096]{0:T(1024)S(1)}, /*index=5*/f32[...) fusion(f32[128,4096]{1,0:T(8,128)} %get-tuple-element.875, ...), kind=kLoop, calls=%fused_computation.1.clone.1 | loop fusion | flops 16711680 | bytes 35913792 | tf_op jit(solution)/shard_map/while/body/eval_jaxpr/reduce_sum | solution.py:189
  760.8 163.7 %while.48 = (s32[]{:T(128)}, f32[128,4096]{1,0:T(8,128)S(1)}, f32[128,4096]{1,0:T(8,128)}, f32[255,4096]{1,0:T(8,128)}, s32[]{:T(128)}, /*index=5*/s32[]{:T(128)...) while((s32[]{:T(128)}, f32[128,4096]{1,0:T(8,128)S(1)}, ...), condition=%wide.region_15.16_spmd.clone, body=%wide.region_14.15_spmd.clone.sunk | while | flops 17301544 | bytes 38535948 | solution.py:176
  763.2 19.1 %fusion.402 = f32[128,4096]{1,0:T(8,128)S(1)} fusion(f32[255,4096]{1,0:T(8,128)} %get-tuple-element.800, s32[]{:T(128)S(6)} %add.1299, s32[]{:T(128)S(6)} %add.1300, s32[]{:T(128)S(6)} %add.1301, s32[]{:T(128)S(6)} %add.1302, s32[]{:T(128)S(6)} %add.1303, s32[]{:T(128)S(6)} %add.1304, s32[]{:T(128)S(6)} %add.1305, s32[]{:T(128)S(6)} %add.1306, ...), kind=kLoop, calls=%fused_computation.82.clone.1 | loop fusion | flops 17301504 | bytes 38010944 | tf_op jit(solution)/shard_map/while/body/eval_jaxpr/add | solution.py:173
  784.8 19.2 %fusion.402 = f32[128,4096]{1,0:T(8,128)S(1)} fusion(f32[255,4096]{1,0:T(8,128)} %get-tuple-element.800, s32[]{:T(128)S(6)} %add.1299, s32[]{:T(128)S(6)} %add.1300, s32[]{:T(128)S(6)} %add.1301, s32[]{:T(128)S(6)} %add.1302, s32[]{:T(128)S(6)} %add.1303, s32[]{:T(128)S(6)} %add.1304, s32[]{:T(128)S(6)} %add.1305, s32[]{:T(128)S(6)} %add.1306, ...), kind=kLoop, calls=%fused_computation.82.clone.1 | loop fusion | flops 17301504 | bytes 38010944 | tf_op jit(solution)/shard_map/while/body/eval_jaxpr/add | solution.py:173
  806.4 17.7 %fusion.402 = f32[128,4096]{1,0:T(8,128)S(1)} fusion(f32[255,4096]{1,0:T(8,128)} %get-tuple-element.800, s32[]{:T(128)S(6)} %add.1299, s32[]{:T(128)S(6)} %add.1300, s32[]{:T(128)S(6)} %add.1301, s32[]{:T(128)S(6)} %add.1302, s32[]{:T(128)S(6)} %add.1303, s32[]{:T(128)S(6)} %add.1304, s32[]{:T(128)S(6)} %add.1305, s32[]{:T(128)S(6)} %add.1306, ...), kind=kLoop, calls=%fused_computation.82.clone.1 | loop fusion | flops 17301504 | bytes 38010944 | tf_op jit(solution)/shard_map/while/body/eval_jaxpr/add | solution.py:173
  826.5 17.1 %fusion.402 = f32[128,4096]{1,0:T(8,128)S(1)} fusion(f32[255,4096]{1,0:T(8,128)} %get-tuple-element.800, s32[]{:T(128)S(6)} %add.1299, s32[]{:T(128)S(6)} %add.1300, s32[]{:T(128)S(6)} %add.1301, s32[]{:T(128)S(6)} %add.1302, s32[]{:T(128)S(6)} %add.1303, s32[]{:T(128)S(6)} %add.1304, s32[]{:T(128)S(6)} %add.1305, s32[]{:T(128)S(6)} %add.1306, ...), kind=kLoop, calls=%fused_computation.82.clone.1 | loop fusion | flops 17301504 | bytes 38010944 | tf_op jit(solution)/shard_map/while/body/eval_jaxpr/add | solution.py:173
  846.4 18.4 %fusion.402 = f32[128,4096]{1,0:T(8,128)S(1)} fusion(f32[255,4096]{1,0:T(8,128)} %get-tuple-element.800, s32[]{:T(128)S(6)} %add.1299, s32[]{:T(128)S(6)} %add.1300, s32[]{:T(128)S(6)} %add.1301, s32[]{:T(128)S(6)} %add.1302, s32[]{:T(128)S(6)} %add.1303, s32[]{:T(128)S(6)} %add.1304, s32[]{:T(128)S(6)} %add.1305, s32[]{:T(128)S(6)} %add.1306, ...), kind=kLoop, calls=%fused_computation.82.clone.1 | loop fusion | flops 17301504 | bytes 38010944 | tf_op jit(solution)/shard_map/while/body/eval_jaxpr/add | solution.py:173
  867.3 17.8 %fusion.402 = f32[128,4096]{1,0:T(8,128)S(1)} fusion(f32[255,4096]{1,0:T(8,128)} %get-tuple-element.800, s32[]{:T(128)S(6)} %add.1299, s32[]{:T(128)S(6)} %add.1300, s32[]{:T(128)S(6)} %add.1301, s32[]{:T(128)S(6)} %add.1302, s32[]{:T(128)S(6)} %add.1303, s32[]{:T(128)S(6)} %add.1304, s32[]{:T(128)S(6)} %add.1305, s32[]{:T(128)S(6)} %add.1306, ...), kind=kLoop, calls=%fused_computation.82.clone.1 | loop fusion | flops 17301504 | bytes 38010944 | tf_op jit(solution)/shard_map/while/body/eval_jaxpr/add | solution.py:173
  887.6 17.6 %fusion.402 = f32[128,4096]{1,0:T(8,128)S(1)} fusion(f32[255,4096]{1,0:T(8,128)} %get-tuple-element.800, s32[]{:T(128)S(6)} %add.1299, s32[]{:T(128)S(6)} %add.1300, s32[]{:T(128)S(6)} %add.1301, s32[]{:T(128)S(6)} %add.1302, s32[]{:T(128)S(6)} %add.1303, s32[]{:T(128)S(6)} %add.1304, s32[]{:T(128)S(6)} %add.1305, s32[]{:T(128)S(6)} %add.1306, ...), kind=kLoop, calls=%fused_computation.82.clone.1 | loop fusion | flops 17301504 | bytes 38010944 | tf_op jit(solution)/shard_map/while/body/eval_jaxpr/add | solution.py:173
  907.4 17.2 %fusion.402 = f32[128,4096]{1,0:T(8,128)S(1)} fusion(f32[255,4096]{1,0:T(8,128)} %get-tuple-element.800, s32[]{:T(128)S(6)} %add.1299, s32[]{:T(128)S(6)} %add.1300, s32[]{:T(128)S(6)} %add.1301, s32[]{:T(128)S(6)} %add.1302, s32[]{:T(128)S(6)} %add.1303, s32[]{:T(128)S(6)} %add.1304, s32[]{:T(128)S(6)} %add.1305, s32[]{:T(128)S(6)} %add.1306, ...), kind=kLoop, calls=%fused_computation.82.clone.1 | loop fusion | flops 17301504 | bytes 38010944 | tf_op jit(solution)/shard_map/while/body/eval_jaxpr/add | solution.py:173
  948.4 5.6 collective-permute-start.20
  958.4 9.1 collective-permute-start.30
  967.6 9.6 collective-permute-start.35
  1002.1 7.1 multiply_convert_fusion.1
  1016.5 5.4 fusion.78
  1026.3 5.4 fusion.80
  1031.7 7.1 multiply_convert_fusion
  (339 shorter events, 273.4 us)
Async XLA Ops:
  7.2 1033.9 %all-reduce.2.cloned.1.call-start = ((), (), s32[]{:S(2)}) async-start(), calls=%async_computation | async-start | bytes 4194304 | tf_op jit(solution)/shard_map/psum | solution.py:195
  8.0 26.7 %collective-permute-start.11 = (f32[1,128]{1,0:T(1,128)S(1)}, f32[1,128]{1,0:T(1,128)S(1)}, u32[]{:S(2)}, u32[]{:S(2)}) collective-permute-start(f32[1,128]{1,0:T(1,128)S(1)} %get-tuple-element.468), channel_id=1, source_target_pairs={{1,0},{2,1},{3,2},{4,3},{5,4},{6,5},{7,6},{8,7},{9,8},{10,9},{11,1... | collective-permute-start | bytes 1544 | tf_op jit(solution)/shard_map/ppermute | solution.py:16
  13.0 30.5 %collective-permute-start.16 = (f32[1,128]{1,0:T(1,128)S(1)}, f32[1,128]{1,0:T(1,128)S(1)}, u32[]{:S(2)}, u32[]{:S(2)}) collective-permute-start(f32[1,128]{1,0:T(1,128)S(1)} %get-tuple-element.468), channel_id=1, source_target_pairs={{2,0},{3,1},{4,2},{5,3},{6,4},{7,5},{8,6},{9,7},{10,8},{11,9},{12,... | collective-permute-start | bytes 1544 | tf_op jit(solution)/shard_map/ppermute | solution.py:16
  15.5 30.2 %collective-permute-start.21 = (f32[1,128]{1,0:T(1,128)S(1)}, f32[1,128]{1,0:T(1,128)S(1)}, u32[]{:S(2)}, u32[]{:S(2)}) collective-permute-start(f32[1,128]{1,0:T(1,128)S(1)} %get-tuple-element.468), channel_id=1, source_target_pairs={{3,0},{4,1},{5,2},{6,3},{7,4},{8,5},{9,6},{10,7},{11,8},{12,9},{13... | collective-permute-start | bytes 1544 | tf_op jit(solution)/shard_map/ppermute | solution.py:16
  18.4 30.1 %collective-permute-start.26 = (f32[1,128]{1,0:T(1,128)S(1)}, f32[1,128]{1,0:T(1,128)S(1)}, u32[]{:S(2)}, u32[]{:S(2)}) collective-permute-start(f32[1,128]{1,0:T(1,128)S(1)} %get-tuple-element.468), channel_id=1, source_target_pairs={{4,0},{5,1},{6,2},{7,3},{8,4},{9,5},{10,6},{11,7},{12,8},{13,9},{1... | collective-permute-start | bytes 1544 | tf_op jit(solution)/shard_map/ppermute | solution.py:16
  25.5 51.9 %collective-permute-start.5 = (bf16[127,4096]{1,0:T(8,128)(2,1)}, bf16[127,4096]{1,0:T(8,128)(2,1)}, u32[]{:S(2)}, u32[]{:S(2)}) collective-permute-start(bf16[127,4096]{1,0:T(8,128)(2,1)} %slice_bitcast_fusion), channel_id=1, source_target_pairs={{0,1},{1,2},{2,3},{3,4},{4,5},{5,6},{6,7},{7,8},{8,9},{9,10},{10,1... | collective-permute-start | bytes 3121160 | tf_op jit(solution)/shard_map/ppermute | solution.py:16
  30.6 267.2 %copy-start.54 = (pred[128,128]{0,1:T(8,128)(4,1)}, pred[128,128]{0,1:T(8,128)(4,1)S(1)}, u32[]{:S(2)}) copy-start(pred[128,128]{0,1:T(8,128)(4,1)S(1)} %get-tuple-element.461) | copy-start | bytes 49156
  30.6 267.7 %copy-start.50 = (pred[128,128]{0,1:T(8,128)(4,1)}, pred[128,128]{0,1:T(8,128)(4,1)S(1)}, u32[]{:S(2)}) copy-start(pred[128,128]{0,1:T(8,128)(4,1)S(1)} %get-tuple-element.466) | copy-start | bytes 49156
  30.6 268.5 %copy-start.48 = (pred[128,128]{0,1:T(8,128)(4,1)}, pred[128,128]{0,1:T(8,128)(4,1)S(1)}, u32[]{:S(2)}) copy-start(pred[128,128]{0,1:T(8,128)(4,1)S(1)} %get-tuple-element.462) | copy-start | bytes 49156
  30.6 269.0 %copy-start.46 = (pred[128,128]{0,1:T(8,128)(4,1)}, pred[128,128]{0,1:T(8,128)(4,1)S(1)}, u32[]{:S(2)}) copy-start(pred[128,128]{0,1:T(8,128)(4,1)S(1)} %get-tuple-element.463) | copy-start | bytes 49156
  30.7 274.1 %copy-start.44 = (pred[128,128]{0,1:T(8,128)(4,1)}, pred[128,128]{0,1:T(8,128)(4,1)S(1)}, u32[]{:S(2)}) copy-start(pred[128,128]{0,1:T(8,128)(4,1)S(1)} %get-tuple-element.464) | copy-start | bytes 49156
  30.7 352.4 %copy-start.52 = (pred[128,128]{0,1:T(8,128)(4,1)}, pred[128,128]{0,1:T(8,128)(4,1)S(1)}, u32[]{:S(2)}) copy-start(pred[128,128]{0,1:T(8,128)(4,1)S(1)} %get-tuple-element.465) | copy-start | bytes 49156
  34.7 15.8 %collective-permute-start.31 = (f32[1,128]{1,0:T(1,128)S(1)}, f32[1,128]{1,0:T(1,128)S(1)}, u32[]{:S(2)}, u32[]{:S(2)}) collective-permute-start(f32[1,128]{1,0:T(1,128)S(1)} %get-tuple-element.468), channel_id=1, source_target_pairs={{5,0},{6,1},{7,2},{8,3},{9,4},{10,5},{11,6},{12,7},{13,8},{14,9},{... | collective-permute-start | bytes 1544 | tf_op jit(solution)/shard_map/ppermute | solution.py:16
  43.5 212.7 %collective-permute-start.4 = (bf16[128,4096]{0,1:T(8,128)(2,1)}, bf16[128,4096]{0,1:T(8,128)(2,1)}, u32[]{:S(2)}, u32[]{:S(2)}) collective-permute-start(bf16[128,4096]{0,1:T(8,128)(2,1)} %bitcast.544), channel_id=1, source_target_pairs={{0,5},{1,6},{2,7},{3,8},{4,9},{5,10},{6,11},{7,12},{8,13},{9,14},{... | collective-permute-start | bytes 3145736 | tf_op jit(solution)/shard_map/ppermute | solution.py:16
  45.8 214.8 %collective-permute-start.3 = (bf16[128,4096]{0,1:T(8,128)(2,1)}, bf16[128,4096]{0,1:T(8,128)(2,1)}, u32[]{:S(2)}, u32[]{:S(2)}) collective-permute-start(bf16[128,4096]{0,1:T(8,128)(2,1)} %bitcast.545), channel_id=1, source_target_pairs={{0,4},{1,5},{2,6},{3,7},{4,8},{5,9},{6,10},{7,11},{8,12},{9,13},{1... | collective-permute-start | bytes 3145736 | tf_op jit(solution)/shard_map/ppermute | solution.py:16
  48.5 219.0 %collective-permute-start.2 = (bf16[128,4096]{0,1:T(8,128)(2,1)}, bf16[128,4096]{0,1:T(8,128)(2,1)}, u32[]{:S(2)}, u32[]{:S(2)}) collective-permute-start(bf16[128,4096]{0,1:T(8,128)(2,1)} %bitcast.546), channel_id=1, source_target_pairs={{0,3},{1,4},{2,5},{3,6},{4,7},{5,8},{6,9},{7,10},{8,11},{9,12},{10... | collective-permute-start | bytes 3145736 | tf_op jit(solution)/shard_map/ppermute | solution.py:16
  50.4 231.3 %collective-permute-start.1 = (bf16[128,4096]{0,1:T(8,128)(2,1)}, bf16[128,4096]{0,1:T(8,128)(2,1)}, u32[]{:S(2)}, u32[]{:S(2)}) collective-permute-start(bf16[128,4096]{0,1:T(8,128)(2,1)} %bitcast.547), channel_id=1, source_target_pairs={{0,2},{1,3},{2,4},{3,5},{4,6},{5,7},{6,8},{7,9},{8,10},{9,11},{10,... | collective-permute-start | bytes 3145736 | tf_op jit(solution)/shard_map/ppermute | solution.py:16
  53.2 471.8 %copy-start.58 = (pred[128,128]{0,1:T(8,128)(4,1)}, pred[128,128]{0,1:T(8,128)(4,1)S(1)}, u32[]{:S(2)}) copy-start(pred[128,128]{0,1:T(8,128)(4,1)S(1)} %get-tuple-element.458) | copy-start | bytes 49156
  53.2 474.7 %copy-start.60 = (pred[128,128]{0,1:T(8,128)(4,1)}, pred[128,128]{0,1:T(8,128)(4,1)S(1)}, u32[]{:S(2)}) copy-start(pred[128,128]{0,1:T(8,128)(4,1)S(1)} %get-tuple-element.457) | copy-start | bytes 49156
  53.2 477.5 %copy-start.56 = (pred[128,128]{0,1:T(8,128)(4,1)}, pred[128,128]{0,1:T(8,128)(4,1)S(1)}, u32[]{:S(2)}) copy-start(pred[128,128]{0,1:T(8,128)(4,1)S(1)} %get-tuple-element.459) | copy-start | bytes 49156
  77.4 208.7 %collective-permute-start = (bf16[128,4096]{0,1:T(8,128)(2,1)}, bf16[128,4096]{0,1:T(8,128)(2,1)}, u32[]{:S(2)}, u32[]{:S(2)}) collective-permute-start(bf16[128,4096]{0,1:T(8,128)(2,1)} %bitcast.548), channel_id=1, source_target_pairs={{0,1},{1,2},{2,3},{3,4},{4,5},{5,6},{6,7},{7,8},{8,9},{9,10},{10,1... | collective-permute-start | bytes 3145736 | tf_op jit(solution)/shard_map/ppermute | solution.py:16
  256.2 44.0 %collective-permute-start.22 = (bf16[128,4096]{0,1:T(8,128)(2,1)}, bf16[128,4096]{0,1:T(8,128)(2,1)S(1)}, u32[]{:S(2)}, u32[]{:S(2)}) collective-permute-start(bf16[128,4096]{0,1:T(8,128)(2,1)} %bitcast.457), channel_id=1, source_target_pairs={{3,0},{4,1},{5,2},{6,3},{7,4},{8,5},{9,6},{10,7},{11,8},{12,9},{13... | collective-permute-start | bytes 3145736 | tf_op jit(solution)/shard_map/ppermute | solution.py:16
  260.6 122.5 %copy-start.8 = (f32[32,128,128]{1,2,0:T(8,128)}, f32[32,128,128]{1,2,0:T(8,128)S(1)}, u32[]{:S(2)}) copy-start(f32[32,128,128]{1,2,0:T(8,128)S(1)} %get-tuple-element.470) | copy-start | bytes 6291460
  260.6 61.8 %collective-permute-start.17 = (bf16[128,4096]{0,1:T(8,128)(2,1)S(1)}, bf16[128,4096]{0,1:T(8,128)(2,1)S(1)}, u32[]{:S(2)}, u32[]{:S(2)}) collective-permute-start(bf16[128,4096]{0,1:T(8,128)(2,1)S(1)} %bitcast.460), channel_id=1, source_target_pairs={{2,0},{3,1},{4,2},{5,3},{6,4},{7,5},{8,6},{9,7},{10,8},{11,9},{12,... | collective-permute-start | bytes 3145736 | tf_op jit(solution)/shard_map/ppermute | solution.py:16
  267.5 116.1 %collective-permute-start.24 = (bf16[128,4096]{1,0:T(8,128)(2,1)}, bf16[128,4096]{1,0:T(8,128)(2,1)S(1)}, u32[]{:S(2)}, u32[]{:S(2)}) collective-permute-start(bf16[128,4096]{1,0:T(8,128)(2,1)} %bitcast.44), channel_id=1, source_target_pairs={{3,0},{4,1},{5,2},{6,3},{7,4},{8,5},{9,6},{10,7},{11,8},{12,9},{13... | collective-permute-start | bytes 3145736 | tf_op jit(solution)/shard_map/ppermute | solution.py:16
  281.8 185.4 %collective-permute-start.19 = (bf16[128,4096]{1,0:T(8,128)(2,1)}, bf16[128,4096]{1,0:T(8,128)(2,1)}, u32[]{:S(2)}, u32[]{:S(2)}) collective-permute-start(bf16[128,4096]{1,0:T(8,128)(2,1)} %bitcast.44), channel_id=1, source_target_pairs={{2,0},{3,1},{4,2},{5,3},{6,4},{7,5},{8,6},{9,7},{10,8},{11,9},{12,... | collective-permute-start | bytes 3145736 | tf_op jit(solution)/shard_map/ppermute | solution.py:16
  286.1 87.4 %collective-permute-start.12 = (bf16[128,4096]{0,1:T(8,128)(2,1)S(1)}, bf16[128,4096]{0,1:T(8,128)(2,1)S(1)}, u32[]{:S(2)}, u32[]{:S(2)}) collective-permute-start(bf16[128,4096]{0,1:T(8,128)(2,1)S(1)} %bitcast.464), channel_id=1, source_target_pairs={{1,0},{2,1},{3,2},{4,3},{5,4},{6,5},{7,6},{8,7},{9,8},{10,9},{11,1... | collective-permute-start | bytes 3145736 | tf_op jit(solution)/shard_map/ppermute | solution.py:16
  300.2 130.1 %collective-permute-start.27 = (bf16[128,4096]{0,1:T(8,128)(2,1)S(1)}, bf16[128,4096]{0,1:T(8,128)(2,1)S(1)}, u32[]{:S(2)}, u32[]{:S(2)}) collective-permute-start(bf16[128,4096]{0,1:T(8,128)(2,1)S(1)} %bitcast.466), channel_id=1, source_target_pairs={{4,0},{5,1},{6,2},{7,3},{8,4},{9,5},{10,6},{11,7},{12,8},{13,9},{1... | collective-permute-start | bytes 3145736 | tf_op jit(solution)/shard_map/ppermute | solution.py:16
  322.4 148.9 %collective-permute-start.14 = (bf16[128,4096]{1,0:T(8,128)(2,1)}, bf16[128,4096]{1,0:T(8,128)(2,1)}, u32[]{:S(2)}, u32[]{:S(2)}) collective-permute-start(bf16[128,4096]{1,0:T(8,128)(2,1)} %bitcast.44), channel_id=1, source_target_pairs={{1,0},{2,1},{3,2},{4,3},{5,4},{6,5},{7,6},{8,7},{9,8},{10,9},{11,1... | collective-permute-start | bytes 3145736 | tf_op jit(solution)/shard_map/ppermute | solution.py:16
  373.5 63.6 %collective-permute-start.32 = (bf16[128,4096]{0,1:T(8,128)(2,1)S(1)}, bf16[128,4096]{0,1:T(8,128)(2,1)S(1)}, u32[]{:S(2)}, u32[]{:S(2)}) collective-permute-start(bf16[128,4096]{0,1:T(8,128)(2,1)S(1)} %bitcast.467), channel_id=1, source_target_pairs={{5,0},{6,1},{7,2},{8,3},{9,4},{10,5},{11,6},{12,7},{13,8},{14,9},{... | collective-permute-start | bytes 3145736 | tf_op jit(solution)/shard_map/ppermute | solution.py:16
  383.6 96.3 %collective-permute-start.29 = (bf16[128,4096]{1,0:T(8,128)(2,1)}, bf16[128,4096]{1,0:T(8,128)(2,1)}, u32[]{:S(2)}, u32[]{:S(2)}) collective-permute-start(bf16[128,4096]{1,0:T(8,128)(2,1)} %bitcast.44), channel_id=1, source_target_pairs={{4,0},{5,1},{6,2},{7,3},{8,4},{9,5},{10,6},{11,7},{12,8},{13,9},{1... | collective-permute-start | bytes 3145736 | tf_op jit(solution)/shard_map/ppermute | solution.py:16
  430.3 61.6 %collective-permute-start.34 = (bf16[128,4096]{1,0:T(8,128)(2,1)}, bf16[128,4096]{1,0:T(8,128)(2,1)}, u32[]{:S(2)}, u32[]{:S(2)}) collective-permute-start(bf16[128,4096]{1,0:T(8,128)(2,1)} %bitcast.44), channel_id=1, source_target_pairs={{5,0},{6,1},{7,2},{8,3},{9,4},{10,5},{11,6},{12,7},{13,8},{14,9},{... | collective-permute-start | bytes 3145736 | tf_op jit(solution)/shard_map/ppermute | solution.py:16
  437.2 87.8 %collective-permute-start.23 = (f32[32,128]{1,0:T(8,128)S(1)}, f32[32,128]{1,0:T(8,128)S(1)}, u32[]{:S(2)}, u32[]{:S(2)}) collective-permute-start(f32[32,128]{1,0:T(8,128)S(1)} %log_add_fusion), channel_id=1, source_target_pairs={{3,0},{4,1},{5,2},{6,3},{7,4},{8,5},{9,6},{10,7},{11,8},{12,9},{13... | collective-permute-start | bytes 49160 | tf_op jit(solution)/shard_map/ppermute | solution.py:16
  467.2 60.7 %collective-permute-start.18 = (f32[32,128]{1,0:T(8,128)S(1)}, f32[32,128]{1,0:T(8,128)S(1)}, u32[]{:S(2)}, u32[]{:S(2)}) collective-permute-start(f32[32,128]{1,0:T(8,128)S(1)} %log_add_fusion), channel_id=1, source_target_pairs={{2,0},{3,1},{4,2},{5,3},{6,4},{7,5},{8,6},{9,7},{10,8},{11,9},{12,... | collective-permute-start | bytes 49160 | tf_op jit(solution)/shard_map/ppermute | solution.py:16
  471.3 57.5 %collective-permute-start.13 = (f32[32,128]{1,0:T(8,128)S(1)}, f32[32,128]{1,0:T(8,128)S(1)}, u32[]{:S(2)}, u32[]{:S(2)}) collective-permute-start(f32[32,128]{1,0:T(8,128)S(1)} %log_add_fusion), channel_id=1, source_target_pairs={{1,0},{2,1},{3,2},{4,3},{5,4},{6,5},{7,6},{8,7},{9,8},{10,9},{11,1... | collective-permute-start | bytes 49160 | tf_op jit(solution)/shard_map/ppermute | solution.py:16
  479.8 50.8 %collective-permute-start.28 = (f32[32,128]{1,0:T(8,128)S(1)}, f32[32,128]{1,0:T(8,128)S(1)}, u32[]{:S(2)}, u32[]{:S(2)}) collective-permute-start(f32[32,128]{1,0:T(8,128)S(1)} %log_add_fusion), channel_id=1, source_target_pairs={{4,0},{5,1},{6,2},{7,3},{8,4},{9,5},{10,6},{11,7},{12,8},{13,9},{1... | collective-permute-start | bytes 49160 | tf_op jit(solution)/shard_map/ppermute | solution.py:16
  491.9 40.7 %collective-permute-start.33 = (f32[32,128]{1,0:T(8,128)S(1)}, f32[32,128]{1,0:T(8,128)S(1)}, u32[]{:S(2)}, u32[]{:S(2)}) collective-permute-start(f32[32,128]{1,0:T(8,128)S(1)} %log_add_fusion), channel_id=1, source_target_pairs={{5,0},{6,1},{7,2},{8,3},{9,4},{10,5},{11,6},{12,7},{13,8},{14,9},{... | collective-permute-start | bytes 49160 | tf_op jit(solution)/shard_map/ppermute | solution.py:16
  544.8 380.9 %collective-permute-start.6 = (bf16[128,4096]{1,0:T(8,128)(2,1)}, bf16[128,4096]{1,0:T(8,128)(2,1)}, u32[]{:S(2)}, u32[]{:S(2)}) collective-permute-start(bf16[128,4096]{1,0:T(8,128)(2,1)} %get-tuple-element.453), channel_id=1, source_target_pairs={{0,1},{1,2},{2,3},{3,4},{4,5},{5,6},{6,7},{7,8},{8,9},{9,10},{10,1... | collective-permute-start | bytes 3145736 | tf_op jit(solution)/shard_map/ppermute | solution.py:16
  548.7 379.8 %collective-permute-start.7 = (bf16[128,4096]{1,0:T(8,128)(2,1)}, bf16[128,4096]{1,0:T(8,128)(2,1)}, u32[]{:S(2)}, u32[]{:S(2)}) collective-permute-start(bf16[128,4096]{1,0:T(8,128)(2,1)} %get-tuple-element.453), channel_id=1, source_target_pairs={{0,2},{1,3},{2,4},{3,5},{4,6},{5,7},{6,8},{7,9},{8,10},{9,11},{10,... | collective-permute-start | bytes 3145736 | tf_op jit(solution)/shard_map/ppermute | solution.py:16
  550.6 380.1 %collective-permute-start.8 = (bf16[128,4096]{1,0:T(8,128)(2,1)}, bf16[128,4096]{1,0:T(8,128)(2,1)}, u32[]{:S(2)}, u32[]{:S(2)}) collective-permute-start(bf16[128,4096]{1,0:T(8,128)(2,1)} %get-tuple-element.453), channel_id=1, source_target_pairs={{0,3},{1,4},{2,5},{3,6},{4,7},{5,8},{6,9},{7,10},{8,11},{9,12},{10... | collective-permute-start | bytes 3145736 | tf_op jit(solution)/shard_map/ppermute | solution.py:16
  552.6 380.3 %collective-permute-start.9 = (bf16[128,4096]{1,0:T(8,128)(2,1)}, bf16[128,4096]{1,0:T(8,128)(2,1)}, u32[]{:S(2)}, u32[]{:S(2)}) collective-permute-start(bf16[128,4096]{1,0:T(8,128)(2,1)} %get-tuple-element.453), channel_id=1, source_target_pairs={{0,4},{1,5},{2,6},{3,7},{4,8},{5,9},{6,10},{7,11},{8,12},{9,13},{1... | collective-permute-start | bytes 3145736 | tf_op jit(solution)/shard_map/ppermute | solution.py:16
  554.5 200.4 %collective-permute-start.36 = (bf16[127,4096]{1,0:T(8,128)(2,1)}, bf16[127,4096]{1,0:T(8,128)(2,1)}, u32[]{:S(2)}, u32[]{:S(2)}) collective-permute-start(bf16[127,4096]{1,0:T(8,128)(2,1)} %bitcast.346), channel_id=1, source_target_pairs={{1,0},{2,1},{3,2},{4,3},{5,4},{6,5},{7,6},{8,7},{9,8},{10,9},{11,1... | collective-permute-start | bytes 3121160 | tf_op jit(solution)/shard_map/ppermute | solution.py:16
  754.9 180.2 %collective-permute-start.10 = (bf16[128,4096]{1,0:T(8,128)(2,1)}, bf16[128,4096]{1,0:T(8,128)(2,1)}, u32[]{:S(2)}, u32[]{:S(2)}) collective-permute-start(bf16[128,4096]{1,0:T(8,128)(2,1)} %get-tuple-element.453), channel_id=1, source_target_pairs={{0,5},{1,6},{2,7},{3,8},{4,9},{5,10},{6,11},{7,12},{8,13},{9,14},{... | collective-permute-start | bytes 3145736 | tf_op jit(solution)/shard_map/ppermute | solution.py:16
  944.8 67.0 %collective-permute-start.15 = (f32[32,128]{1,0:T(8,128)S(1)}, f32[32,128]{1,0:T(8,128)S(1)}, u32[]{:S(2)}, u32[]{:S(2)}) collective-permute-start(f32[32,128]{1,0:T(8,128)S(1)} %copy.149), channel_id=1, source_target_pairs={{1,0},{2,1},{3,2},{4,3},{5,4},{6,5},{7,6},{8,7},{9,8},{10,9},{11,1... | collective-permute-start | bytes 49160 | tf_op jit(solution)/shard_map/ppermute | solution.py:16
  948.4 68.0 %collective-permute-start.20 = (f32[32,128]{1,0:T(8,128)S(1)}, f32[32,128]{1,0:T(8,128)S(1)}, u32[]{:S(2)}, u32[]{:S(2)}) collective-permute-start(f32[32,128]{1,0:T(8,128)S(1)} %copy.149), channel_id=1, source_target_pairs={{2,0},{3,1},{4,2},{5,3},{6,4},{7,5},{8,6},{9,7},{10,8},{11,9},{12,... | collective-permute-start | bytes 49160 | tf_op jit(solution)/shard_map/ppermute | solution.py:16
  954.0 67.9 %collective-permute-start.25 = (f32[32,128]{1,0:T(8,128)S(1)}, f32[32,128]{1,0:T(8,128)S(1)}, u32[]{:S(2)}, u32[]{:S(2)}) collective-permute-start(f32[32,128]{1,0:T(8,128)S(1)} %copy.149), channel_id=1, source_target_pairs={{3,0},{4,1},{5,2},{6,3},{7,4},{8,5},{9,6},{10,7},{11,8},{12,9},{13... | collective-permute-start | bytes 49160 | tf_op jit(solution)/shard_map/ppermute | solution.py:16
  958.4 67.8 %collective-permute-start.30 = (f32[32,128]{1,0:T(8,128)S(1)}, f32[32,128]{1,0:T(8,128)S(1)}, u32[]{:S(2)}, u32[]{:S(2)}) collective-permute-start(f32[32,128]{1,0:T(8,128)S(1)} %copy.149), channel_id=1, source_target_pairs={{4,0},{5,1},{6,2},{7,3},{8,4},{9,5},{10,6},{11,7},{12,8},{13,9},{1... | collective-permute-start | bytes 49160 | tf_op jit(solution)/shard_map/ppermute | solution.py:16
  967.6 64.1 %collective-permute-start.35 = (f32[32,128]{1,0:T(8,128)S(1)}, f32[32,128]{1,0:T(8,128)S(1)}, u32[]{:S(2)}, u32[]{:S(2)}) collective-permute-start(f32[32,128]{1,0:T(8,128)S(1)} %copy.149), channel_id=1, source_target_pairs={{5,0},{6,1},{7,2},{8,3},{9,4},{10,5},{11,6},{12,7},{13,8},{14,9},{... | collective-permute-start | bytes 49160 | tf_op jit(solution)/shard_map/ppermute | solution.py:16
  (70 other events, 536.2 us)
Sparse Core Ops, SparseCore 0:
  748.6 161.4 all-reduce.1
where the time goes:
time: 1070 us; the launch traced here: 1050 us
  other arithmetic  475 us (44%)
  starting transfers between devices  252 us (24%)
  matrix products  110 us (10%)
  local copies, waits for them, and re-layouts  104 us (10%)
  waiting for transfers between devices  88.6 us (8%)
  between operations  15.9 us (1%)
    ppermute x37, starting transfers between devices, passed_along(): return lax.ppermute(x, axis, pairs)  252 us
    reduce_sum x8, other arithmetic, group_sums(): rows_out.append(jnp.sum(grad_local * region[lead:lead + tok_rows], 0))  157 us
    add x8, other arithmetic, add_group(): summed = summed + block_taps[inner][None, :] * region[lead:lead + tok_rows]  153 us
    add x8, other arithmetic, back_group(): summed + block_taps[inner][None, :] * region[inner:inner + tok_rows]  144 us
    ppermute x37, waiting for transfers between devices, passed_along(): return lax.ppermute(x, axis, pairs)  88.5 us
    dot_general x6, matrix products, query_step(): jnp.einsum('hij,ihe->jhe', dscore, query_piece, preferred_element_type=jn...  30.8 us
    dot_general x6, matrix products, on_device(): jnp.einsum('hij,jhe->ihe', dscore, key_split, preferred_element_type=jnp....  27.9 us
  transfers between devices with their start and end apart: 38, of which 3 were waited for; matrix products, arithmetic and copies ran while one was open for 64% of the time, Pallas kernels for 0%

commit v1 on v0

v1 whole, which is shorter than its diff:
```python
import functools

import jax
import jax.numpy as jnp
from jax import lax
from jax.experimental import pallas as pl
from jax.experimental.pallas import tpu as pltpu
from jax.sharding import PartitionSpec as P


HEADS = 32
LANES = 128
PAD = 5
QT = 2
WINDOWS = (3, 5, 7)
LOG2E = 1.4426950408889634
F32 = jnp.float32
BF16 = jnp.bfloat16


def contract(a, b, da, db):
    return lax.dot_general(a, b, (((da,), (db,)), ((), ())), preferred_element_type=F32)


def pack_values(values, doc_start):
    blocks = HEADS
    step = 4

    def body(v_ref, d_ref, o_ref):
        doc = jnp.broadcast_to(d_ref[...], (16, LANES))
        row = lax.broadcasted_iota(jnp.int32, (16, LANES), 0)
        high = lax.shift_right_logical(doc, 8)
        low = jnp.bitwise_and(doc, 255)
        info = jnp.where(row == 0, high, jnp.where(row == 1, low, 0)).astype(F32).astype(BF16)
        for h in range(step):
            o_ref[h, 0:LANES] = v_ref[:, h * LANES : (h + 1) * LANES]
            o_ref[h, LANES : LANES + 16] = info

    return pl.pallas_call(
        body,
        grid=(blocks // step,),
        in_specs=[
            pl.BlockSpec((LANES, step * LANES), lambda i: (0, i)),
            pl.BlockSpec((1, LANES), lambda i: (0, 0)),
        ],
        out_specs=pl.BlockSpec((step, LANES + 16, LANES), lambda i: (i, 0, 0)),
        out_shape=jax.ShapeDtypeStruct((blocks, LANES + 16, LANES), BF16),
        cost_estimate=pl.CostEstimate(flops=0, bytes_accessed=2 << 20, transcendentals=0),
        name="pack_values",
    )(values, doc_start)


def pack_many(*arrays):
    count = len(arrays)
    step = 4

    def body(*refs):
        o_ref = refs[-1]
        for a in range(count):
            for h in range(step):
                o_ref[h, a] = refs[a][:, h * LANES : (h + 1) * LANES]

    return pl.pallas_call(
        body,
        grid=(HEADS // step,),
        in_specs=[pl.BlockSpec((LANES, step * LANES), lambda i: (0, i))] * count,
        out_specs=pl.BlockSpec((step, count, LANES, LANES), lambda i: (i, 0, 0, 0)),
        out_shape=jax.ShapeDtypeStruct((HEADS, count, LANES, LANES), BF16),
        cost_estimate=pl.CostEstimate(flops=0, bytes_accessed=count << 21, transcendentals=0),
        name="pack_many",
    )(*arrays)


def unpack_many(packed, count, types):
    step = 4

    def body(*refs):
        for a in range(count):
            for h in range(step):
                refs[1 + a][:, h * LANES : (h + 1) * LANES] = refs[0][h, a].astype(types[a])

    return pl.pallas_call(
        body,
        grid=(HEADS // step,),
        in_specs=[pl.BlockSpec((step, count, LANES, LANES), lambda i: (i, 0, 0, 0))],
        out_specs=[pl.BlockSpec((LANES, step * LANES), lambda i: (0, i))] * count,
        out_shape=[jax.ShapeDtypeStruct((LANES, HEADS * LANES), t) for t in types],
        cost_estimate=pl.CostEstimate(flops=0, bytes_accessed=count << 21, transcendentals=0),
        name="unpack_many",
    )(packed)


def toeplitz(wt, c):
    w = wt[pl.ds(c, 1), :]
    z = jnp.concatenate([w, jnp.zeros((1, LANES), F32)], 1)
    rows = pltpu.roll(jnp.broadcast_to(z, (LANES, 2 * LANES)), 0, 1, stride=1, stride_axis=0)
    high = rows.astype(BF16)
    low = (rows - high.astype(F32)).astype(BF16)
    return high, low


SLOT = 40


def conv_forward(me, recv, filter_taps):
    blocks = recv.shape[0]

    def body(me_ref, v_ref, taps_ref, mixed_ref, xt, yt, wt):
        wt[...] = taps_ref[...].T

        def clear(c, carry):
            xt[pl.ds(c * SLOT, 8), :] = jnp.zeros((8, LANES), F32)
            return carry

        lax.fori_loop(0, LANES, clear, 0, unroll=8)
        for b in range(blocks):
            xt[pl.ds(8 + b, LANES, stride=SLOT), :] = v_ref[b].astype(F32).T

        def channel(c, carry):
            high, low = toeplitz(wt, c)
            rhs = jnp.concatenate(
                [
                    jnp.concatenate([high[:, :LANES], low[:, :LANES]], 1),
                    jnp.concatenate([high[:, LANES:], low[:, LANES:]], 1),
                ],
                0,
            )
            now = xt[pl.ds(c * SLOT + 8, blocks), :]
            back = xt[pl.ds(c * SLOT + 7, blocks), :]
            lhs = jnp.concatenate([now, back], 1).astype(BF16)
            y = jnp.dot(lhs, rhs, preferred_element_type=F32)
            yt[pl.ds(c * blocks, blocks), :] = y[:, :LANES] + y[:, LANES:]
            return carry

        lax.fori_loop(0, LANES, channel, 0, unroll=4)
        for b in range(blocks):
            mixed_ref[b] = yt[pl.ds(b, LANES, stride=blocks), :].T

    return pl.pallas_call(
        body,
        grid_spec=pltpu.PrefetchScalarGridSpec(
            num_scalar_prefetch=1,
            grid=(1,),
            in_specs=[
                pl.BlockSpec((blocks, LANES, LANES), lambda i, m: (0, 0, 0)),
                pl.BlockSpec((LANES, LANES), lambda i, m: (0, m[0])),
            ],
            out_specs=pl.BlockSpec((blocks, LANES, LANES), lambda i, m: (0, 0, 0)),
            scratch_shapes=[
                pltpu.VMEM((LANES * SLOT, LANES), F32),
                pltpu.VMEM((LANES * blocks, LANES), F32),
                pltpu.VMEM((LANES, LANES), F32),
            ],
        ),
        out_shape=jax.ShapeDtypeStruct((blocks, LANES, LANES), F32),
        cost_estimate=pl.CostEstimate(
            flops=2 * LANES * blocks * 256 * 256 * 4, bytes_accessed=4 << 20, transcendentals=0
        ),
        name="conv_forward",
    )(me, recv, filter_taps)


def attention(need, packed, recv, mixed):
    blocks = packed.shape[0]
    rows = (blocks + PAD) * LANES
    scale = LANES ** (-0.5)
    factor = scale * LOG2E
    width = QT * LANES
    tiles = blocks // QT

    def body(need_ref, q_ref, k_ref, g_ref, d_ref, info_ref, mixed_ref, out_ref, gm_ref, ks, hs, kt, dk, dv, st):
        pad = PAD * LANES
        ks[0:pad, :] = jnp.zeros((pad, LANES), BF16)
        hs[0:pad, :] = jnp.zeros((pad, LANES), BF16)
        kt[:, 0:pad] = jnp.zeros((LANES, pad), BF16)
        dk[...] = jnp.zeros_like(dk)
        dv[...] = jnp.zeros_like(dv)
        for b in range(blocks):
            at = pad + b * LANES
            key = k_ref[b]
            ks[at : at + LANES, :] = key
            kt[:, at : at + LANES] = key.T
            hs[at : at + LANES, :] = (g_ref[b].astype(F32) * mixed_ref[b]).astype(BF16)
            info = info_ref[b].astype(F32)
            st[b // QT, 0:1, (b % QT) * LANES : (b % QT + 1) * LANES] = info[0:1] * 256.0 + info[1:2]

        def tile(i, window):
            span = window * LANES
            first = pl.multiple_of((QT * i + QT - window) * LANES + pad, LANES)
            q = q_ref[pl.ds(QT * i, QT)].reshape(width, LANES)
            d = d_ref[pl.ds(QT * i, QT)].reshape(width, LANES)
            start = st[i, 0:1, :].astype(jnp.int32) - (first - pad)
            s = contract(ks[pl.ds(first, span), :], q, 1, 1)
            kpos = lax.broadcasted_iota(jnp.int32, (span, width), 0)
            qpos = lax.broadcasted_iota(jnp.int32, (span, width), 1) + (window - QT) * LANES
            allowed = (kpos >= start) & (kpos <= qpos)
            s = jnp.where(allowed, s, -1e30)
            top = jnp.max(s, 0, keepdims=True) * factor
            p = jnp.exp2(s * factor - top)
            p = p * (1.0 / jnp.sum(p, 0, keepdims=True))
            half = p.astype(BF16)
            dp = contract(hs[pl.ds(first, span), :], d, 1, 1)
            delta = jnp.sum(half.astype(F32) * dp, 0, keepdims=True)
            ds = (p * (dp - delta)).astype(BF16)
            dv[pl.ds(first, span), :] += jnp.dot(half, d, preferred_element_type=F32)
            dk[pl.ds(first, span), :] += jnp.dot(ds, q, preferred_element_type=F32)
            dq = jnp.dot(kt[:, pl.ds(first, span)], ds, preferred_element_type=F32) * scale
            for j in range(QT):
                out_ref[QT * i + j, 0] = dq[:, j * LANES : (j + 1) * LANES].T.astype(BF16)

        def step(i, carry):
            count = need_ref[i]
            low = 0
            for window in WINDOWS:
                pl.when((count > low) & (count <= window))(functools.partial(tile, i, window))
                low = window
            return carry

        lax.fori_loop(0, tiles, step, 0)
        for b in range(blocks):
            at = pad + b * LANES
            out_ref[b, 1] = (dk[at : at + LANES, :] * scale).astype(BF16)
            gh = dv[at : at + LANES, :]
            out_ref[b, 2] = (gh * mixed_ref[b]).astype(BF16)
            gm_ref[b] = (gh * g_ref[b].astype(F32)).astype(BF16)

    def piece(a):
        return pl.BlockSpec((blocks, None, LANES, LANES), lambda i, n: (0, a, 0, 0))

    whole = pl.BlockSpec((blocks, LANES, LANES), lambda i, n: (0, 0, 0))
    return pl.pallas_call(
        body,
        grid_spec=pltpu.PrefetchScalarGridSpec(
            num_scalar_prefetch=1,
            grid=(1,),
            in_specs=[piece(0), piece(1), piece(2), piece(3),
                      pl.BlockSpec((blocks, 16, LANES), lambda i, n: (0, 8, 0)), whole],
            out_specs=[pl.BlockSpec((blocks, 3, LANES, LANES), lambda i, n: (0, 0, 0, 0)), whole],
            scratch_shapes=[
                pltpu.VMEM((rows, LANES), BF16),
                pltpu.VMEM((rows, LANES), BF16),
                pltpu.VMEM((LANES, rows), BF16),
                pltpu.VMEM((rows, LANES), F32),
                pltpu.VMEM((rows, LANES), F32),
                pltpu.VMEM((tiles, 8, width), F32),
            ],
        ),
        out_shape=[
            jax.ShapeDtypeStruct((blocks, 3, LANES, LANES), BF16),
            jax.ShapeDtypeStruct((blocks, LANES, LANES), BF16),
        ],
        cost_estimate=pl.CostEstimate(
            flops=10 * 896 * 4096 * 128, bytes_accessed=10 << 20, transcendentals=896 * 4096
        ),
        name="attention",
    )(need, packed, packed, packed, packed, recv, mixed)


def conv_backward(me, grad_mixed, recv, filter_taps):
    blocks = recv.shape[0]

    def body(me_ref, gm_ref, v_ref, taps_ref, out_ref, gf_ref, xt, gt, yt, wt, at):
        wt[...] = taps_ref[...].T

        def clear(c, carry):
            xt[pl.ds(c * SLOT, 8), :] = jnp.zeros((8, LANES), F32)
            gt[pl.ds(c * SLOT + blocks, 8), :] = jnp.zeros((8, LANES), F32)
            return carry

        lax.fori_loop(0, LANES, clear, 0, unroll=8)
        for b in range(blocks):
            xt[pl.ds(8 + b, LANES, stride=SLOT), :] = v_ref[b].astype(F32).T
            gt[pl.ds(b, LANES, stride=SLOT), :] = gm_ref[b].astype(F32).T
        t_at = lax.broadcasted_iota(jnp.int32, (LANES, LANES), 0)
        s_at = lax.broadcasted_iota(jnp.int32, (LANES, LANES), 1)
        lower = s_at <= t_at

        def channel(c, carry):
            high, low = toeplitz(wt, c)
            rhs = jnp.concatenate([high, low], 0)
            now = gt[pl.ds(c * SLOT, blocks), :].astype(BF16)
            after = gt[pl.ds(c * SLOT + 1, blocks), :].astype(BF16)
            y = contract(jnp.concatenate([now, after], 1), rhs, 1, 1)
            yt[pl.ds(c * blocks, blocks), :] = y[:, :LANES] + y[:, LANES:]
            value = xt[pl.ds(c * SLOT + 8, blocks), :]
            back = xt[pl.ds(c * SLOT + 7, blocks), :]
            m = contract(now, jnp.concatenate([value, back], 1).astype(BF16), 0, 0)
            d = jnp.where(lower, m[:, :LANES], m[:, LANES:])
            total = d[0:8]
            for j in range(1, LANES // 8):
                total = total + pltpu.roll(d[8 * j : 8 * j + 8], LANES - 8 * j, 1)
            at[pl.ds(c * 8, 8), :] = total
            return carry

        lax.fori_loop(0, LANES, channel, 0, unroll=4)
        for b in range(blocks):
            out_ref[b, 0] = yt[pl.ds(b, LANES, stride=blocks), :].T.astype(BF16)
        total = at[pl.ds(0, LANES, stride=8), :]
        for r in range(1, 8):
            total = total + pltpu.roll(at[pl.ds(r, LANES, stride=8), :], LANES - r, 1)
        flip = jnp.where(s_at == jnp.bitwise_and(LANES - t_at, LANES - 1), 1.0, 0.0).astype(F32)
        gf_ref[...] = lax.dot_general(
            flip, total, (((1,), (1,)), ((), ())), precision=lax.Precision.HIGHEST,
            preferred_element_type=F32,
        )

    return pl.pallas_call(
        body,
        grid_spec=pltpu.PrefetchScalarGridSpec(
            num_scalar_prefetch=1,
            grid=(1,),
            in_specs=[
                pl.BlockSpec((blocks, LANES, LANES), lambda i, m: (0, 0, 0)),
                pl.BlockSpec((blocks, LANES, LANES), lambda i, m: (0, 0, 0)),
                pl.BlockSpec((LANES, LANES), lambda i, m: (0, m[0])),
            ],
            out_specs=[
                pl.BlockSpec((blocks, 1, LANES, LANES), lambda i, m: (0, 0, 0, 0)),
                pl.BlockSpec((LANES, LANES), lambda i, m: (0, 0)),
            ],
            scratch_shapes=[
                pltpu.VMEM((LANES * SLOT, LANES), F32),
                pltpu.VMEM((LANES * SLOT, LANES), F32),
                pltpu.VMEM((LANES * blocks, LANES), F32),
                pltpu.VMEM((LANES, LANES), F32),
                pltpu.VMEM((LANES * 8, LANES), F32),
            ],
        ),
        out_shape=[
            jax.ShapeDtypeStruct((blocks, 2, LANES, LANES), BF16),
            jax.ShapeDtypeStruct((LANES, LANES), F32),
        ],
        cost_estimate=pl.CostEstimate(
            flops=2 * LANES * blocks * 256 * 256 * 4, bytes_accessed=4 << 20, transcendentals=0
        ),
        name="conv_backward",
    )(me, grad_mixed, recv, filter_taps)


def exchange(packed):
    return lax.all_to_all(packed, "ctx", 0, 0, tiled=True)


def on_device(queries, keys, gate, values, grad_out, doc_start, filter_taps):
    me = lax.axis_index("ctx").astype(jnp.int32)[None]
    recv = exchange(pack_values(values[0], doc_start))
    packed = exchange(pack_many(queries[0], keys[0], gate[0], grad_out[0]))
    mixed = conv_forward(me, recv, filter_taps)
    blocks = recv.shape[0]
    info = recv[:, LANES : LANES + 2, 0].astype(jnp.int32)
    starts = info[:, 0] * 256 + info[:, 1]
    first = starts[::QT]
    need = QT * jnp.arange(1, blocks // QT + 1, dtype=jnp.int32) - first // LANES
    grads, grad_mixed = attention(need, packed, recv, mixed)
    grads = exchange(grads)
    last, grad_taps = conv_backward(me, grad_mixed, recv, filter_taps)
    grad_taps = grad_taps + lax.ppermute(grad_taps, "dp", [(0, 1), (1, 0), (2, 3), (3, 2)])
    grad_taps = grad_taps + lax.ppermute(grad_taps, "dp", [(0, 2), (2, 0), (1, 3), (3, 1)])
    last = last.at[:, 1].set(jnp.broadcast_to(grad_taps.astype(BF16)[None], (blocks, LANES, LANES)))
    last = exchange(last)
    grad_query, grad_key, grad_gate = unpack_many(grads, 3, (BF16, BF16, BF16))
    grad_values, grad_filter = unpack_many(last, 2, (BF16, F32))
    return grad_query[None], grad_key[None], grad_gate[None], grad_values[None], grad_filter


def solution(mesh):
    placed = P("dp", "ctx", None)
    return jax.shard_map(
        on_device,
        mesh=mesh,
        in_specs=(placed, placed, placed, placed, placed, P("dp", "ctx"), P()),
        out_specs=(placed, placed, placed, placed, P()),
        check_vma=False,
    )
```

time: 1070 us -> 237 us (0.22)
  the two profiles are of different devices: /device:TPU:100 before, /device:TPU:6 now
where the time goes in v1:
time: 237 us; the launch traced here: 236 us
  waiting for transfers between devices  90.9 us (38%)
  Pallas kernels  81.1 us (34%)
  blocking collectives  36.8 us (16%)
  starting transfers between devices  21.7 us (9%)
  local copies, waits for them, and re-layouts  3.04 us (1%)
    all_to_all x3, waiting for transfers between devices, exchange(): return lax.all_to_all(packed, 'ctx', 0, 0, tiled=True)  85.2 us
    all_to_all x1, blocking collectives, exchange(): return lax.all_to_all(packed, 'ctx', 0, 0, tiled=True)  36.8 us
    pallas_call x1, Pallas kernels, attention(): pl.pallas_call(body, grid_spec=pltpu.PrefetchScalarGridSpec(num_scalar_pr...  22.8 us
    all_to_all x3, starting transfers between devices, exchange(): return lax.all_to_all(packed, 'ctx', 0, 0, tiled=True)  21.6 us
    pallas_call x1, Pallas kernels, conv_backward(): pl.pallas_call(body, grid_spec=pltpu.PrefetchScalarGridSpec(num_scalar_pr...  19.8 us
    pallas_call x1, Pallas kernels, conv_forward(): pl.pallas_call(body, grid_spec=pltpu.PrefetchScalarGridSpec(num_scalar_pr...  14.2 us
    pallas_call x2, Pallas kernels, unpack_many(): pl.pallas_call(body, grid=(HEADS // step,), in_specs=[pl.BlockSpec((step,...  12.1 us
    pallas_call x1, Pallas kernels, pack_many(): pl.pallas_call(body, grid=(HEADS // step,), in_specs=[pl.BlockSpec((LANES...  6.93 us
  transfers between devices with their start and end apart: 5, of which 5 were waited for; matrix products, arithmetic and copies ran while one was open for 0% of the time, Pallas kernels for 11%

profile of v1, /device:TPU:6, one launch (start us, length us, event | category | flops | bytes accessed | tf_op | source)
XLA Modules:
  0.0 235.6 jit_solution(890869926448144062)
XLA Ops:
  0.6 5.3 %pack_values.1 = bf16[32,144,128]{2,1,0:T(8,128)(2,1)} custom-call(bf16[128,4096]{1,0:T(8,128)(2,1)} %bitcast.13, s32[1,128]{1,0:T(1,128)} %d_ref.1), custom_call_target="tpu_custom_call" | custom-call | bytes 2097152 | tf_op jit(solution)/shard_map/pack_values/pallas_call | solution.py:39
  5.9 10.9 %all-to-all-start = ((bf16[32,144,128]{2,1,0:T(8,128)(2,1)}), bf16[32,144,128]{2,1,0:T(8,128)(2,1)S(1)}, u32[]{:S(2)}, u32[]{:S(2)}) async-start(bf16[32,144,128]{2,1,0:T(8,128)(2,1)} %pack_values.1), calls=%async_computation | async-start | bytes 2359296 | tf_op jit(solution)/shard_map/all_to_all | solution.py:341
  16.8 6.9 %pack_many.1 = bf16[32,4,128,128]{3,2,1,0:T(8,128)(2,1)} custom-call(bf16[128,4096]{1,0:T(8,128)(2,1)} %bitcast.14, bf16[128,4096]{1,0:T(8,128)(2,1)} %bitcast.15, bf16[128,4096]{1,0:T(8,128)(2,1)} %bitcast.16, bf16[128,4096]{1,0:T(8,128)(2,1)} %bitcast.17), custom_call_target="tpu_custom_call" | custom-call | bytes 8388608 | tf_op jit(solution)/shard_map/pack_many/pallas_call | solution.py:63
  23.7 11.9 %all-to-all-done.v_ref.info_ref = bf16[32,144,128]{2,1,0:T(8,128)(2,1)S(1)} async-done(((bf16[32,144,128]{2,1,0:T(8,128)(2,1)}), bf16[32,144,128]{2,1,0:T(8,128)(2,1)S(1)}, u32[]{:S(2)}, u32[]{:S(2)}) %all-to-all-start) | async-done | bytes 1179680 | tf_op jit(solution)/shard_map/all_to_all | solution.py:341
  35.7 0.0 copy-start.1
  35.7 5.4 %all-to-all-start.1 = ((bf16[32,4,128,128]{3,2,1,0:T(8,128)(2,1)}), bf16[32,4,128,128]{3,2,1,0:T(8,128)(2,1)}, u32[]{:S(2)}, u32[]{:S(2)}) async-start(bf16[32,4,128,128]{3,2,1,0:T(8,128)(2,1)} %pack_many.1), calls=%async_computation.1 | async-start | bytes 8388608 | tf_op jit(solution)/shard_map/all_to_all | solution.py:341
  41.1 0.0 copy-done.1
  41.1 0.1 copy.13
  41.2 0.1 slice.40
  41.4 14.2 %conv_forward.1.mixed_ref = f32[32,128,128]{2,1,0:T(8,128)} custom-call(s32[1]{0:T(128)} %bitcast.7.me_ref, bf16[32,144,128]{2,1,0:T(8,128)(2,1)} %copy-done.1, f32[128,4096]{1,0:T(8,128)} %taps_ref.3), custom_call_target="tpu_custom_call" | custom-call | flops 2147483648 | bytes 4194304 | tf_op jit(solution)/shard_map/conv_forward/pallas_call | solution.py:139
  55.5 0.5 fusion.need_ref
  56.1 37.6 %all-to-all-done.1.q_ref.k_ref.g_ref.d_ref = bf16[32,4,128,128]{3,2,1,0:T(8,128)(2,1)} async-done(((bf16[32,4,128,128]{3,2,1,0:T(8,128)(2,1)}), bf16[32,4,128,128]{3,2,1,0:T(8,128)(2,1)}, u32[]{:S(2)}, u32[]{:S(2)}) %all-to-all-start.1) | async-done | bytes 4194336 | tf_op jit(solution)/shard_map/all_to_all | solution.py:341
  93.6 22.8 %attention.1 = (bf16[32,3,128,128]{3,2,1,0:T(8,128)(2,1)}, bf16[32,128,128]{2,1,0:T(8,128)(2,1)}) custom-call(s32[16]{0:T(128)} %fusion.need_ref, bf16[32,4,128,128]{3,2,1,0:T(8,128)(2,1)} %all-to-all-done.1.q_ref.k_ref.g_ref.d_ref, bf16[32,4,128,128]{3,2,1,0:T(8,128)(2,1)} %all-to-all-done.1.q_ref.k_ref.g_ref.d_ref, ...), custom_call_target="tpu_custom_call" | custom-call | flops 4697620480 | bytes 10485760 | tf_op jit(solution)/shard_map/attention/pallas_call | solution.py:231
  116.4 19.8 %conv_backward.1 = (bf16[32,2,128,128]{3,2,1,0:T(8,128)(2,1)}, f32[128,128]{1,0:T(8,128)}) custom-call(s32[1]{0:T(128)} %bitcast.7.me_ref, bf16[32,128,128]{2,1,0:T(8,128)(2,1)} %get-tuple-element.30.gm_ref, bf16[32,144,128]{2,1,0:T(8,128)(2,1)} %copy-done.1, f32[128,4096]{1,0:T(8,128)} %taps_ref.3), custom_call_target="tpu_custom_call" | custom-call | flops 2147483648 | bytes 4194304 | tf_op jit(solution)/shard_map/conv_backward/pallas_call | solution.py:307
  136.2 0.0 collective-permute-start
  136.2 1.5 collective-permute-done
  137.7 0.9 add.21
  138.5 0.1 collective-permute-start.1
  138.6 4.3 %collective-permute-done.1 = f32[128,128]{1,0:T(8,128)S(1)} collective-permute-done((f32[128,128]{1,0:T(8,128)S(1)}, f32[128,128]{1,0:T(8,128)S(1)}, u32[]{:S(2)}, u32[]{:S(2)}) %collective-permute-start.1) | collective-permute-done | bytes 65568 | tf_op jit(solution)/shard_map/ppermute | solution.py:358
  142.9 1.2 broadcast_dynamic-update-slice_fusion
  144.1 36.8 %all_to_all.20.refs_0_ = bf16[32,2,128,128]{3,2,1,0:T(8,128)(2,1)} all-to-all(bf16[32,2,128,128]{3,2,1,0:T(8,128)(2,1)} %broadcast_dynamic-update-slice_fusion), channel_id=1, replica_groups=mesh['dp'=4,'ctx'=32] {'ctx'}, dimensions={0} | all-to-all | bytes 4194304 | tf_op jit(solution)/shard_map/all_to_all | solution.py:341
  180.8 5.3 %all-to-all-start.2 = ((bf16[32,3,128,128]{3,2,1,0:T(8,128)(2,1)}), bf16[32,3,128,128]{3,2,1,0:T(8,128)(2,1)S(1)}, u32[]{:S(2)}, u32[]{:S(2)}) async-start(bf16[32,3,128,128]{3,2,1,0:T(8,128)(2,1)} %get-tuple-element.26), calls=%async_computation.2 | async-start | bytes 6291456 | tf_op jit(solution)/shard_map/all_to_all | solution.py:341
  186.2 5.9 %unpack_many.3 = (bf16[128,4096]{1,0:T(8,128)(2,1)}, f32[128,4096]{1,0:T(8,128)}) custom-call(bf16[32,2,128,128]{3,2,1,0:T(8,128)(2,1)} %all_to_all.20.refs_0_), custom_call_target="tpu_custom_call" | custom-call | bytes 4194304 | tf_op jit(solution)/shard_map/unpack_many/pallas_call | solution.py:82
  192.1 35.7 %all-to-all-done.2.refs_0_ = bf16[32,3,128,128]{3,2,1,0:T(8,128)(2,1)S(1)} async-done(((bf16[32,3,128,128]{3,2,1,0:T(8,128)(2,1)}), bf16[32,3,128,128]{3,2,1,0:T(8,128)(2,1)S(1)}, u32[]{:S(2)}, u32[]{:S(2)}) %all-to-all-start.2) | async-done | bytes 3145760 | tf_op jit(solution)/shard_map/all_to_all | solution.py:341
  227.8 0.0 copy-start
  227.8 1.6 copy-done
  229.4 6.3 %unpack_many.2 = (bf16[128,4096]{1,0:T(8,128)(2,1)}, bf16[128,4096]{1,0:T(8,128)(2,1)}, bf16[128,4096]{1,0:T(8,128)(2,1)}) custom-call(bf16[32,3,128,128]{3,2,1,0:T(8,128)(2,1)} %copy-done), custom_call_target="tpu_custom_call" | custom-call | bytes 6291456 | tf_op jit(solution)/shard_map/unpack_many/pallas_call | solution.py:82
  (3 shorter events, 0.0 us)
Async XLA Ops:
  5.9 29.8 %all-to-all-start = ((bf16[32,144,128]{2,1,0:T(8,128)(2,1)}), bf16[32,144,128]{2,1,0:T(8,128)(2,1)S(1)}, u32[]{:S(2)}, u32[]{:S(2)}) async-start(bf16[32,144,128]{2,1,0:T(8,128)(2,1)} %pack_values.1), calls=%async_computation | async-start | bytes 2359296 | tf_op jit(solution)/shard_map/all_to_all | solution.py:341
  35.7 5.4 %copy-start.1 = (bf16[32,144,128]{2,1,0:T(8,128)(2,1)}, bf16[32,144,128]{2,1,0:T(8,128)(2,1)S(1)}, u32[]{:S(2)}) copy-start(bf16[32,144,128]{2,1,0:T(8,128)(2,1)S(1)} %all-to-all-done.v_ref.info_ref) | copy-start | bytes 3538948
  35.7 58.0 %all-to-all-start.1 = ((bf16[32,4,128,128]{3,2,1,0:T(8,128)(2,1)}), bf16[32,4,128,128]{3,2,1,0:T(8,128)(2,1)}, u32[]{:S(2)}, u32[]{:S(2)}) async-start(bf16[32,4,128,128]{3,2,1,0:T(8,128)(2,1)} %pack_many.1), calls=%async_computation.1 | async-start | bytes 8388608 | tf_op jit(solution)/shard_map/all_to_all | solution.py:341
  136.2 1.5 collective-permute-start
  138.5 4.3 %collective-permute-start.1 = (f32[128,128]{1,0:T(8,128)S(1)}, f32[128,128]{1,0:T(8,128)S(1)}, u32[]{:S(2)}, u32[]{:S(2)}) collective-permute-start(f32[128,128]{1,0:T(8,128)S(1)} %add.21), channel_id=1, source_target_pairs={{0,64},{64,0},{32,96},{96,32},{1,65},{65,1},{33,97},{97,33},{2,66}... | collective-permute-start | bytes 196616 | tf_op jit(solution)/shard_map/ppermute | solution.py:358
  180.8 46.9 %all-to-all-start.2 = ((bf16[32,3,128,128]{3,2,1,0:T(8,128)(2,1)}), bf16[32,3,128,128]{3,2,1,0:T(8,128)(2,1)S(1)}, u32[]{:S(2)}, u32[]{:S(2)}) async-start(bf16[32,3,128,128]{3,2,1,0:T(8,128)(2,1)} %get-tuple-element.26), calls=%async_computation.2 | async-start | bytes 6291456 | tf_op jit(solution)/shard_map/all_to_all | solution.py:341
  227.8 1.6 copy-start

commit v2 on v1

v2 whole, which is shorter than its diff:
```python
import functools

import jax
import jax.numpy as jnp
from jax import lax
from jax.experimental import pallas as pl
from jax.experimental.pallas import tpu as pltpu
from jax.sharding import PartitionSpec as P


HEADS = 32
LANES = 128
PAD = 5
QT = 2
TWIN = 2
WINDOWS = (2, 3, 4, 5, 6, 7)
LOG2E = 1.4426950408889634
F32 = jnp.float32
BF16 = jnp.bfloat16


def contract(a, b, da, db):
    return lax.dot_general(a, b, (((da,), (db,)), ((), ())), preferred_element_type=F32)


def pack(arrays, doc_start=None):
    count = len(arrays)
    step = HEADS // 2
    extra = 0 if doc_start is None else INFO

    def body(*refs):
        o_ref = refs[-1]
        for a in range(count):
            for h in range(step):
                o_ref[h, a * LANES : (a + 1) * LANES] = refs[a][:, h * LANES : (h + 1) * LANES]
        if extra:
            doc = jnp.broadcast_to(refs[count][...], (INFO, LANES))
            row = lax.broadcasted_iota(jnp.int32, (INFO, LANES), 0)
            high = lax.shift_right_logical(doc, 8)
            low = jnp.bitwise_and(doc, 255)
            info = jnp.where(row == 0, high, jnp.where(row == 1, low, 0)).astype(F32).astype(BF16)
            for h in range(step):
                o_ref[h, count * LANES : count * LANES + INFO] = info

    rows = count * LANES + extra
    specs = [pl.BlockSpec((LANES, step * LANES), lambda i: (0, i))] * count
    if extra:
        arrays = arrays + (doc_start,)
        specs = specs + [pl.BlockSpec((1, LANES), lambda i: (0, 0))]
    return pl.pallas_call(
        body,
        grid=(HEADS // step,),
        in_specs=specs,
        out_specs=pl.BlockSpec((step, rows, LANES), lambda i: (i, 0, 0)),
        out_shape=jax.ShapeDtypeStruct((HEADS, rows, LANES), BF16),
        cost_estimate=pl.CostEstimate(flops=0, bytes_accessed=count << 21, transcendentals=0),
        name="pack",
    )(*arrays)


def unpack(packed, types):
    count = len(types)
    step = HEADS // 2

    def body(*refs):
        for a in range(count):
            for h in range(step):
                piece = refs[0][h, a * LANES : (a + 1) * LANES]
                refs[1 + a][:, h * LANES : (h + 1) * LANES] = piece.astype(types[a])

    return pl.pallas_call(
        body,
        grid=(HEADS // step,),
        in_specs=[pl.BlockSpec((step, count * LANES, LANES), lambda i: (i, 0, 0))],
        out_specs=[pl.BlockSpec((LANES, step * LANES), lambda i: (0, i))] * count,
        out_shape=[jax.ShapeDtypeStruct((LANES, HEADS * LANES), t) for t in types],
        cost_estimate=pl.CostEstimate(flops=0, bytes_accessed=count << 21, transcendentals=0),
        compiler_params=pltpu.CompilerParams(vmem_limit_bytes=SMALL),
        name="unpack",
    )(packed)


def toeplitz(wt, c):
    w = wt[pl.ds(c, 1), :]
    z = jnp.concatenate([w, jnp.zeros((1, LANES), F32)], 1)
    rows = pltpu.roll(jnp.broadcast_to(z, (LANES, 2 * LANES)), 0, 1, stride=1, stride_axis=0)
    high = rows.astype(BF16)
    low = (rows - high.astype(F32)).astype(BF16)
    return high, low


SLOT = 40
INFO = 8
SMALL = 24 << 20


def conv_forward(me, recv, filter_taps):
    blocks = recv.shape[0]

    def body(me_ref, v_ref, taps_ref, mixed_ref, xt, yt, wt):
        wt[...] = taps_ref[...].T

        def clear(c, carry):
            xt[pl.ds(c * SLOT, 8), :] = jnp.zeros((8, LANES), F32)
            return carry

        lax.fori_loop(0, LANES, clear, 0, unroll=8)
        for b in range(blocks):
            xt[pl.ds(8 + b, LANES, stride=SLOT), :] = v_ref[b].T.astype(F32)

        def channel(c, carry):
            high, low = toeplitz(wt, c)
            rhs = jnp.concatenate(
                [
                    jnp.concatenate([high[:, :LANES], low[:, :LANES]], 1),
                    jnp.concatenate([high[:, LANES:], low[:, LANES:]], 1),
                ],
                0,
            )
            now = xt[pl.ds(c * SLOT + 8, blocks), :]
            back = xt[pl.ds(c * SLOT + 7, blocks), :]
            lhs = jnp.concatenate([now, back], 1).astype(BF16)
            y = jnp.dot(lhs, rhs, preferred_element_type=F32)
            yt[pl.ds(c * blocks, blocks), :] = y[:, :LANES] + y[:, LANES:]
            return carry

        lax.fori_loop(0, LANES, channel, 0, unroll=4)
        for b in range(blocks):
            mixed_ref[b] = yt[pl.ds(b, LANES, stride=blocks), :].T

    return pl.pallas_call(
        body,
        grid_spec=pltpu.PrefetchScalarGridSpec(
            num_scalar_prefetch=1,
            grid=(1,),
            in_specs=[
                pl.BlockSpec((blocks, LANES, LANES), lambda i, m: (0, 0, 0)),
                pl.BlockSpec((LANES, LANES), lambda i, m: (0, m[0])),
            ],
            out_specs=pl.BlockSpec((blocks, LANES, LANES), lambda i, m: (0, 0, 0)),
            scratch_shapes=[
                pltpu.VMEM((LANES * SLOT, LANES), F32),
                pltpu.VMEM((LANES * blocks, LANES), F32),
                pltpu.VMEM((LANES, LANES), F32),
            ],
        ),
        out_shape=jax.ShapeDtypeStruct((blocks, LANES, LANES), F32),
        cost_estimate=pl.CostEstimate(
            flops=2 * LANES * blocks * 256 * 256 * 4, bytes_accessed=4 << 20, transcendentals=0
        ),
        name="conv_forward",
    )(me, recv, filter_taps)


CHUNK = 8
FLUSH = TWIN * QT


def attention(need, packed, recv, mixed):
    blocks = packed.shape[0]
    rows = (blocks + PAD) * LANES
    scale = LANES ** (-0.5)
    factor = scale * LOG2E
    width = QT * LANES
    tiles = blocks // QT
    chunks = blocks // CHUNK
    steps = tiles // TWIN
    pad = PAD * LANES

    def body(need_ref, packed_ref, info_ref, mixed_hbm, out_hbm, gm_hbm,
             q_ref, k_ref, g_ref, d_ref, mixed_ref, out_ref, gm_ref, ks, hs, kt, dk, dv, st, in_sem, out_sem):
        def arrivals(c):
            at = pl.ds(c * CHUNK, CHUNK)
            moves = []
            for a, ref in enumerate((q_ref, k_ref, g_ref, d_ref)):
                source = packed_ref.at[at, pl.ds(a * LANES, LANES)]
                moves.append(pltpu.make_async_copy(source, ref.at[at], in_sem.at[c, a]))
            moves.append(pltpu.make_async_copy(mixed_hbm.at[at], mixed_ref.at[at], in_sem.at[c, 4]))
            return moves

        def departures(f):
            at = pl.ds(f * FLUSH, FLUSH)
            return [
                pltpu.make_async_copy(out_ref.at[at], out_hbm.at[at], out_sem.at[f, 0]),
                pltpu.make_async_copy(gm_ref.at[at], gm_hbm.at[at], out_sem.at[f, 1]),
            ]

        for c in range(chunks):
            for move in arrivals(c):
                move.start()
        ks[0:pad, :] = jnp.zeros((pad, LANES), BF16)
        hs[0:pad, :] = jnp.zeros((pad, LANES), BF16)
        kt[:, 0:pad] = jnp.zeros((LANES, pad), BF16)
        dk[...] = jnp.zeros_like(dk)
        dv[...] = jnp.zeros_like(dv)
        for b in range(blocks):
            info = info_ref[b].astype(F32)
            st[b // QT, 0:1, (b % QT) * LANES : (b % QT + 1) * LANES] = info[0:1] * 256.0 + info[1:2]

        def prepare(c):
            for move in arrivals(c):
                move.wait()
            for u in range(CHUNK):
                b = c * CHUNK + u
                at = pl.multiple_of(pad + b * LANES, LANES)
                key = k_ref[b]
                ks[pl.ds(at, LANES), :] = key
                kt[:, pl.ds(at, LANES)] = key.T
                hs[pl.ds(at, LANES), :] = (g_ref[b].astype(F32) * mixed_ref[b]).astype(BF16)

        def finish(f):
            for u in range(FLUSH):
                b = f * FLUSH + u
                at = pl.multiple_of(pad + b * LANES, LANES)
                out_ref[b, LANES : 2 * LANES] = (dk[pl.ds(at, LANES), :] * scale).astype(BF16)
                gh = dv[pl.ds(at, LANES), :]
                out_ref[b, 2 * LANES : 3 * LANES] = (gh * mixed_ref[b]).astype(BF16)
                gm_ref[b] = (gh * g_ref[b].astype(F32)).astype(BF16)
            for move in departures(f):
                move.start()

        def tiles_of(g, window):
            span = window * LANES
            kpos = lax.broadcasted_iota(jnp.int32, (span, width), 0)
            qpos = lax.broadcasted_iota(jnp.int32, (span, width), 1) + (window - QT) * LANES
            held = []
            for u in range(TWIN):
                i = TWIN * g + u
                first = pl.multiple_of((QT * i + QT - window) * LANES + pad, LANES)
                q = q_ref[pl.ds(QT * i, QT)].reshape(width, LANES)
                d = d_ref[pl.ds(QT * i, QT)].reshape(width, LANES)
                start = st[i, 0:1, :].astype(jnp.int32) - (first - pad)
                s = contract(ks[pl.ds(first, span), :], q, 1, 1)
                s = jnp.where((kpos >= start) & (kpos <= qpos), s, -1e30)
                top = jnp.max(s, 0, keepdims=True) * factor
                p = jnp.exp2(s * factor - top)
                p = p * (1.0 / jnp.sum(p, 0, keepdims=True))
                half = p.astype(BF16)
                dp = contract(hs[pl.ds(first, span), :], d, 1, 1)
                delta = jnp.sum(half.astype(F32) * dp, 0, keepdims=True)
                ds = (p * (dp - delta)).astype(BF16)
                held.append((i, first, q, d, half, ds))
            for i, first, q, d, half, ds in held:
                dq = jnp.dot(kt[:, pl.ds(first, span)], ds, preferred_element_type=F32) * scale
                for j in range(QT):
                    out_ref[QT * i + j, 0:LANES] = dq[:, j * LANES : (j + 1) * LANES].T.astype(BF16)
            for i, first, q, d, half, ds in held:
                dv[pl.ds(first, span), :] += jnp.dot(half, d, preferred_element_type=F32)
                dk[pl.ds(first, span), :] += jnp.dot(ds, q, preferred_element_type=F32)

        def step(g, carry):
            pl.when(g % (CHUNK // FLUSH) == 0)(lambda: prepare(g // (CHUNK // FLUSH)))
            count = need_ref[TWIN * g]
            for u in range(1, TWIN):
                count = jnp.maximum(count, need_ref[TWIN * g + u])
            low = 0
            for window in WINDOWS:
                pl.when((count > low) & (count <= window))(functools.partial(tiles_of, g, window))
                low = window
            pl.when(g >= 2)(lambda: finish(g - 2))
            return carry

        lax.fori_loop(0, steps, step, 0)
        for f in range(steps - 2, steps):
            finish(f)
        for f in range(steps):
            for move in departures(f):
                move.wait()

    anywhere = pl.BlockSpec(memory_space=pl.ANY)
    piece = pltpu.VMEM((blocks, LANES, LANES), BF16)
    return pl.pallas_call(
        body,
        grid_spec=pltpu.PrefetchScalarGridSpec(
            num_scalar_prefetch=1,
            grid=(1,),
            in_specs=[anywhere, pl.BlockSpec((blocks, INFO, LANES), lambda i, n: (0, LANES // INFO, 0)), anywhere],
            out_specs=[anywhere, anywhere],
            scratch_shapes=[
                piece,
                piece,
                piece,
                piece,
                pltpu.VMEM((blocks, LANES, LANES), F32),
                pltpu.VMEM((blocks, 3 * LANES, LANES), BF16),
                piece,
                pltpu.VMEM((rows, LANES), BF16),
                pltpu.VMEM((rows, LANES), BF16),
                pltpu.VMEM((LANES, rows), BF16),
                pltpu.VMEM((rows, LANES), F32),
                pltpu.VMEM((rows, LANES), F32),
                pltpu.VMEM((tiles, 8, width), F32),
                pltpu.SemaphoreType.DMA((chunks, 5)),
                pltpu.SemaphoreType.DMA((steps, 2)),
            ],
        ),
        out_shape=[
            jax.ShapeDtypeStruct((blocks, 3 * LANES, LANES), BF16),
            jax.ShapeDtypeStruct((blocks, LANES, LANES), BF16),
        ],
        cost_estimate=pl.CostEstimate(
            flops=10 * 896 * 4096 * 128, bytes_accessed=10 << 20, transcendentals=896 * 4096
        ),
        name="attention",
    )(need, packed, recv, mixed)


def conv_backward(me, grad_mixed, recv, filter_taps):
    blocks = recv.shape[0]

    def body(me_ref, gm_ref, v_ref, taps_ref, out_ref, gf_ref, xt, gt, yt, wt, at):
        wt[...] = taps_ref[...].T

        def clear(c, carry):
            xt[pl.ds(c * SLOT, 8), :] = jnp.zeros((8, LANES), F32)
            gt[pl.ds(c * SLOT + blocks, 8), :] = jnp.zeros((8, LANES), F32)
            return carry

        lax.fori_loop(0, LANES, clear, 0, unroll=8)
        for b in range(blocks):
            xt[pl.ds(8 + b, LANES, stride=SLOT), :] = v_ref[b].T.astype(F32)
            gt[pl.ds(b, LANES, stride=SLOT), :] = gm_ref[b].T.astype(F32)
        t_at = lax.broadcasted_iota(jnp.int32, (LANES, LANES), 0)
        s_at = lax.broadcasted_iota(jnp.int32, (LANES, LANES), 1)
        lower = s_at <= t_at

        def channel(c, carry):
            high, low = toeplitz(wt, c)
            rhs = jnp.concatenate([high, low], 0)
            now = gt[pl.ds(c * SLOT, blocks), :].astype(BF16)
            after = gt[pl.ds(c * SLOT + 1, blocks), :].astype(BF16)
            y = contract(jnp.concatenate([now, after], 1), rhs, 1, 1)
            yt[pl.ds(c * blocks, blocks), :] = y[:, :LANES] + y[:, LANES:]
            value = xt[pl.ds(c * SLOT + 8, blocks), :]
            back = xt[pl.ds(c * SLOT + 7, blocks), :]
            m = contract(now, jnp.concatenate([value, back], 1).astype(BF16), 0, 0)
            d = jnp.where(lower, m[:, :LANES], m[:, LANES:])
            total = d[0:8]
            for j in range(1, LANES // 8):
                total = total + pltpu.roll(d[8 * j : 8 * j + 8], LANES - 8 * j, 1)
            at[pl.ds(c * 8, 8), :] = total
            return carry

        lax.fori_loop(0, LANES, channel, 0, unroll=4)
        for b in range(blocks):
            out_ref[b] = yt[pl.ds(b, LANES, stride=blocks), :].T.astype(BF16)
        total = at[pl.ds(0, LANES, stride=8), :]
        for r in range(1, 8):
            total = total + pltpu.roll(at[pl.ds(r, LANES, stride=8), :], LANES - r, 1)
        flip = jnp.where(s_at == jnp.bitwise_and(LANES - t_at, LANES - 1), 1.0, 0.0).astype(F32)
        gf_ref[...] = lax.dot_general(
            flip, total, (((1,), (1,)), ((), ())), precision=lax.Precision.HIGHEST,
            preferred_element_type=F32,
        )

    return pl.pallas_call(
        body,
        grid_spec=pltpu.PrefetchScalarGridSpec(
            num_scalar_prefetch=1,
            grid=(1,),
            in_specs=[
                pl.BlockSpec((blocks, LANES, LANES), lambda i, m: (0, 0, 0)),
                pl.BlockSpec((blocks, LANES, LANES), lambda i, m: (0, 0, 0)),
                pl.BlockSpec((LANES, LANES), lambda i, m: (0, m[0])),
            ],
            out_specs=[
                pl.BlockSpec((blocks, LANES, LANES), lambda i, m: (0, 0, 0)),
                pl.BlockSpec((LANES, LANES), lambda i, m: (0, 0)),
            ],
            scratch_shapes=[
                pltpu.VMEM((LANES * SLOT, LANES), F32),
                pltpu.VMEM((LANES * SLOT, LANES), F32),
                pltpu.VMEM((LANES * blocks, LANES), F32),
                pltpu.VMEM((LANES, LANES), F32),
                pltpu.VMEM((LANES * 8, LANES), F32),
            ],
        ),
        out_shape=[
            jax.ShapeDtypeStruct((blocks, 2 * LANES, LANES), BF16),
            jax.ShapeDtypeStruct((LANES, LANES), F32),
        ],
        cost_estimate=pl.CostEstimate(
            flops=2 * LANES * blocks * 256 * 256 * 4, bytes_accessed=4 << 20, transcendentals=0
        ),
        name="conv_backward",
    )(me, grad_mixed, recv, filter_taps)


def exchange(packed):
    return lax.all_to_all(packed, "ctx", 0, 0, tiled=True)


def on_device(queries, keys, gate, values, grad_out, doc_start, filter_taps):
    me = lax.axis_index("ctx").astype(jnp.int32)[None]
    recv = exchange(pack((values[0],), doc_start))
    packed = exchange(pack((queries[0], keys[0], gate[0], grad_out[0])))
    mixed = conv_forward(me, recv, filter_taps)
    blocks = recv.shape[0]
    info = recv[:, LANES : LANES + 2, 0].astype(jnp.int32)
    starts = info[:, 0] * 256 + info[:, 1]
    first = starts[::QT]
    need = QT * jnp.arange(1, blocks // QT + 1, dtype=jnp.int32) - first // LANES
    grads, grad_mixed = attention(need, packed, recv, mixed)
    grads = exchange(grads)
    last, grad_taps = conv_backward(me, grad_mixed, recv, filter_taps)
    grad_taps = grad_taps + lax.ppermute(grad_taps, "dp", [(0, 1), (1, 0), (2, 3), (3, 2)])
    grad_taps = grad_taps + lax.ppermute(grad_taps, "dp", [(0, 2), (2, 0), (1, 3), (3, 1)])
    shared = jnp.broadcast_to(grad_taps.astype(BF16)[None], (blocks, LANES, LANES))
    last = exchange(last.at[:, LANES:].set(shared))
    grad_query, grad_key, grad_gate = unpack(grads, (BF16, BF16, BF16))
    grad_values, grad_filter = unpack(last, (BF16, F32))
    return grad_query[None], grad_key[None], grad_gate[None], grad_values[None], grad_filter


def solution(mesh):
    placed = P("dp", "ctx", None)
    return jax.shard_map(
        on_device,
        mesh=mesh,
        in_specs=(placed, placed, placed, placed, placed, P("dp", "ctx"), P()),
        out_specs=(placed, placed, placed, placed, P()),
        check_vma=False,
    )
```

time: 237 us -> 224 us (0.945)
  Pallas kernels: 81.1 us -> 63.7 us
  waiting for transfers between devices: 90.9 us -> 95.1 us
    pallas_call x4, Pallas kernels: 24.4 us -> 9.95 us  [the longest x2 6.02 us: pack(): pl.pallas_call(body, grid=(HEADS // step,), in_specs=specs, out_specs=pl....]
    all_to_all x3, waiting for transfers between devices: 85.2 us -> 89.9 us  [exchange(): return lax.all_to_all(packed, 'ctx', 0, 0, tiled=True)]
    pallas_call x1, Pallas kernels: 22.8 us -> 19.2 us  [attention(): pl.pallas_call(body, grid_spec=pltpu.PrefetchScalarGridSpec(num_scalar_pr...]
  transfers between devices with their start and end apart: 5 -> 5, of which waited for: 5 -> 5; matrix products, arithmetic and copies ran while one was open for 0% -> 0% of each run, Pallas kernels for 11% -> 9%
where the time goes in v2:
time: 224 us; the launch traced here: 223 us
  waiting for transfers between devices  95.1 us (42%)
  Pallas kernels  63.7 us (28%)
  blocking collectives  36.9 us (16%)
  starting transfers between devices  22.2 us (10%)
  local copies, waits for them, and re-layouts  3 us (1%)
    all_to_all x3, waiting for transfers between devices, exchange(): return lax.all_to_all(packed, 'ctx', 0, 0, tiled=True)  89.9 us
    all_to_all x1, blocking collectives, exchange(): return lax.all_to_all(packed, 'ctx', 0, 0, tiled=True)  36.9 us
    all_to_all x3, starting transfers between devices, exchange(): return lax.all_to_all(packed, 'ctx', 0, 0, tiled=True)  21.6 us
    pallas_call x1, Pallas kernels, conv_backward(): pl.pallas_call(body, grid_spec=pltpu.PrefetchScalarGridSpec(num_scalar_pr...  20.3 us
    pallas_call x1, Pallas kernels, attention(): pl.pallas_call(body, grid_spec=pltpu.PrefetchScalarGridSpec(num_scalar_pr...  19.2 us
    pallas_call x1, Pallas kernels, conv_forward(): pl.pallas_call(body, grid_spec=pltpu.PrefetchScalarGridSpec(num_scalar_pr...  14.2 us
    pallas_call x2, Pallas kernels, pack(): pl.pallas_call(body, grid=(HEADS // step,), in_specs=specs, out_specs=pl....  6.02 us
  transfers between devices with their start and end apart: 5, of which 5 were waited for; matrix products, arithmetic and copies ran while one was open for 0% of the time, Pallas kernels for 9%

profile of v2, /device:TPU:6, one launch (start us, length us, event | category | flops | bytes accessed | tf_op | source)
XLA Modules:
  0.0 223.0 jit_solution(14098015944288763665)
XLA Ops:
  0.6 2.1 pack.2
  2.8 10.9 %all-to-all-start = ((bf16[32,136,128]{2,1,0:T(8,128)(2,1)}), bf16[32,136,128]{2,1,0:T(8,128)(2,1)S(1)}, u32[]{:S(2)}, u32[]{:S(2)}) async-start(bf16[32,136,128]{2,1,0:T(8,128)(2,1)} %pack.2), calls=%async_computation | async-start | bytes 2228224 | tf_op jit(solution)/shard_map/all_to_all | solution.py:390
  13.7 3.9 %pack.3 = bf16[32,512,128]{2,1,0:T(8,128)(2,1)} custom-call(bf16[128,4096]{1,0:T(8,128)(2,1)} %bitcast.14, bf16[128,4096]{1,0:T(8,128)(2,1)} %bitcast.15, bf16[128,4096]{1,0:T(8,128)(2,1)} %bitcast.16, bf16[128,4096]{1,0:T(8,128)(2,1)} %bitcast.17), custom_call_target="tpu_custom_call" | custom-call | bytes 8388608 | tf_op jit(solution)/shard_map/pack/pallas_call | solution.py:50
  17.5 14.3 %all-to-all-done.v_ref.info_ref = bf16[32,136,128]{2,1,0:T(8,128)(2,1)S(1)} async-done(((bf16[32,136,128]{2,1,0:T(8,128)(2,1)}), bf16[32,136,128]{2,1,0:T(8,128)(2,1)S(1)}, u32[]{:S(2)}, u32[]{:S(2)}) %all-to-all-start) | async-done | bytes 1114144 | tf_op jit(solution)/shard_map/all_to_all | solution.py:390
  31.8 0.0 copy-start.1
  31.8 5.4 %all-to-all-start.1 = ((bf16[32,512,128]{2,1,0:T(8,128)(2,1)}), bf16[32,512,128]{2,1,0:T(8,128)(2,1)}, u32[]{:S(2)}, u32[]{:S(2)}) async-start(bf16[32,512,128]{2,1,0:T(8,128)(2,1)} %pack.3), calls=%async_computation.1 | async-start | bytes 8388608 | tf_op jit(solution)/shard_map/all_to_all | solution.py:390
  37.2 0.0 copy-done.1
  37.3 0.1 copy.13
  37.4 0.1 slice.37
  37.5 14.2 %conv_forward.1.mixed_hbm = f32[32,128,128]{2,1,0:T(8,128)} custom-call(s32[1]{0:T(128)} %bitcast.7.me_ref, bf16[32,136,128]{2,1,0:T(8,128)(2,1)} %copy-done.1, f32[128,4096]{1,0:T(8,128)} %taps_ref.3), custom_call_target="tpu_custom_call" | custom-call | flops 2147483648 | bytes 4194304 | tf_op jit(solution)/shard_map/conv_forward/pallas_call | solution.py:131
  51.7 0.5 fusion.need_ref
  52.2 37.5 %all-to-all-done.1.packed_ref = bf16[32,512,128]{2,1,0:T(8,128)(2,1)} async-done(((bf16[32,512,128]{2,1,0:T(8,128)(2,1)}), bf16[32,512,128]{2,1,0:T(8,128)(2,1)}, u32[]{:S(2)}, u32[]{:S(2)}) %all-to-all-start.1) | async-done | bytes 4194336 | tf_op jit(solution)/shard_map/all_to_all | solution.py:390
  89.7 19.2 %attention.1 = (bf16[32,384,128]{2,1,0:T(8,128)(2,1)}, bf16[32,128,128]{2,1,0:T(8,128)(2,1)}) custom-call(s32[16]{0:T(128)} %fusion.need_ref, bf16[32,512,128]{2,1,0:T(8,128)(2,1)} %all-to-all-done.1.packed_ref, bf16[32,136,128]{2,1,0:T(8,128)(2,1)} %copy-done.1, f32[32,128,128]{2,1,0:T(8,128)} %conv_forward.1.mixed_hbm), custom_call_target="tpu_custom_call" | custom-call | flops 4697620480 | bytes 10485760 | tf_op jit(solution)/shard_map/attention/pallas_call | solution.py:272
  108.9 20.3 %conv_backward.1 = (bf16[32,256,128]{2,1,0:T(8,128)(2,1)}, f32[128,128]{1,0:T(8,128)}) custom-call(s32[1]{0:T(128)} %bitcast.7.me_ref, bf16[32,128,128]{2,1,0:T(8,128)(2,1)} %get-tuple-element.30.gm_ref, bf16[32,136,128]{2,1,0:T(8,128)(2,1)} %copy-done.1, f32[128,4096]{1,0:T(8,128)} %taps_ref.3), custom_call_target="tpu_custom_call" | custom-call | flops 2147483648 | bytes 4194304 | tf_op jit(solution)/shard_map/conv_backward/pallas_call | solution.py:356
  129.2 0.0 collective-permute-start
  129.2 1.5 collective-permute-done
  130.7 0.9 add.21
  131.6 0.6 collective-permute-start.1
  132.1 3.8 %collective-permute-done.1 = f32[128,128]{1,0:T(8,128)S(1)} collective-permute-done((f32[128,128]{1,0:T(8,128)S(1)}, f32[128,128]{1,0:T(8,128)S(1)}, u32[]{:S(2)}, u32[]{:S(2)}) %collective-permute-start.1) | collective-permute-done | bytes 65568 | tf_op jit(solution)/shard_map/ppermute | solution.py:407
  135.9 1.2 broadcast_dynamic-update-slice_fusion
  137.1 36.9 %all_to_all.20.refs_0_ = bf16[32,256,128]{2,1,0:T(8,128)(2,1)} all-to-all(bf16[32,256,128]{2,1,0:T(8,128)(2,1)} %broadcast_dynamic-update-slice_fusion), channel_id=1, replica_groups=mesh['dp'=4,'ctx'=32] {'ctx'}, dimensions={0} | all-to-all | bytes 4194304 | tf_op jit(solution)/shard_map/all_to_all | solution.py:390
  174.1 5.3 %all-to-all-start.2 = ((bf16[32,384,128]{2,1,0:T(8,128)(2,1)}), bf16[32,384,128]{2,1,0:T(8,128)(2,1)S(1)}, u32[]{:S(2)}, u32[]{:S(2)}) async-start(bf16[32,384,128]{2,1,0:T(8,128)(2,1)} %get-tuple-element.26), calls=%async_computation.2 | async-start | bytes 6291456 | tf_op jit(solution)/shard_map/all_to_all | solution.py:390
  179.4 0.0 copy-start
  179.4 1.6 copy-done
  181.0 1.9 unpack.3
  182.9 38.1 %all-to-all-done.2.refs_0_ = bf16[32,384,128]{2,1,0:T(8,128)(2,1)S(1)} async-done(((bf16[32,384,128]{2,1,0:T(8,128)(2,1)}), bf16[32,384,128]{2,1,0:T(8,128)(2,1)S(1)}, u32[]{:S(2)}, u32[]{:S(2)}) %all-to-all-start.2) | async-done | bytes 3145760 | tf_op jit(solution)/shard_map/all_to_all | solution.py:390
  221.0 2.1 unpack.2
  (3 shorter events, 0.0 us)
Async XLA Ops:
  2.8 29.1 %all-to-all-start = ((bf16[32,136,128]{2,1,0:T(8,128)(2,1)}), bf16[32,136,128]{2,1,0:T(8,128)(2,1)S(1)}, u32[]{:S(2)}, u32[]{:S(2)}) async-start(bf16[32,136,128]{2,1,0:T(8,128)(2,1)} %pack.2), calls=%async_computation | async-start | bytes 2228224 | tf_op jit(solution)/shard_map/all_to_all | solution.py:390
  31.8 5.4 %copy-start.1 = (bf16[32,136,128]{2,1,0:T(8,128)(2,1)}, bf16[32,136,128]{2,1,0:T(8,128)(2,1)S(1)}, u32[]{:S(2)}) copy-start(bf16[32,136,128]{2,1,0:T(8,128)(2,1)S(1)} %all-to-all-done.v_ref.info_ref) | copy-start | bytes 3342340
  31.8 57.9 %all-to-all-start.1 = ((bf16[32,512,128]{2,1,0:T(8,128)(2,1)}), bf16[32,512,128]{2,1,0:T(8,128)(2,1)}, u32[]{:S(2)}, u32[]{:S(2)}) async-start(bf16[32,512,128]{2,1,0:T(8,128)(2,1)} %pack.3), calls=%async_computation.1 | async-start | bytes 8388608 | tf_op jit(solution)/shard_map/all_to_all | solution.py:390
  129.2 1.5 collective-permute-start
  131.6 4.3 %collective-permute-start.1 = (f32[128,128]{1,0:T(8,128)S(1)}, f32[128,128]{1,0:T(8,128)S(1)}, u32[]{:S(2)}, u32[]{:S(2)}) collective-permute-start(f32[128,128]{1,0:T(8,128)S(1)} %add.21), channel_id=1, source_target_pairs={{0,64},{64,0},{32,96},{96,32},{1,65},{65,1},{33,97},{97,33},{2,66}... | collective-permute-start | bytes 196616 | tf_op jit(solution)/shard_map/ppermute | solution.py:407
  174.1 46.9 %all-to-all-start.2 = ((bf16[32,384,128]{2,1,0:T(8,128)(2,1)}), bf16[32,384,128]{2,1,0:T(8,128)(2,1)S(1)}, u32[]{:S(2)}, u32[]{:S(2)}) async-start(bf16[32,384,128]{2,1,0:T(8,128)(2,1)} %get-tuple-element.26), calls=%async_computation.2 | async-start | bytes 6291456 | tf_op jit(solution)/shard_map/all_to_all | solution.py:390
  179.4 1.6 copy-start

commit v3 on v2

--- a/solution.py
+++ b/solution.py
@@ -91,6 +91,7 @@
 
 SLOT = 40
 INFO = 8
+HALF = LANES // 2
 SMALL = 24 << 20
 
 
@@ -376,14 +377,44 @@
             ],
         ),
         out_shape=[
-            jax.ShapeDtypeStruct((blocks, 2 * LANES, LANES), BF16),
+            jax.ShapeDtypeStruct((blocks, LANES + HALF, LANES), BF16),
             jax.ShapeDtypeStruct((LANES, LANES), F32),
         ],
         cost_estimate=pl.CostEstimate(
             flops=2 * LANES * blocks * 256 * 256 * 4, bytes_accessed=4 << 20, transcendentals=0
         ),
+        compiler_params=pltpu.CompilerParams(vmem_limit_bytes=63 << 20),
         name="conv_backward",
     )(me, grad_mixed, recv, filter_taps)
+
+
+def join_taps(core, last, other):
+    step = HEADS // 2
+
+    def body(core_ref, mine_ref, other_ref, out_ref):
+        at = pl.multiple_of(core_ref[0] * HALF, HALF)
+        rest = pl.multiple_of(HALF - at, HALF)
+        for h in range(step):
+            lanes = slice(h * LANES, (h + 1) * LANES)
+            out_ref[pl.ds(at, HALF), lanes] = mine_ref[h].astype(F32)
+            out_ref[pl.ds(rest, HALF), lanes] = other_ref[h].astype(F32)
+
+    return pl.pallas_call(
+        body,
+        grid_spec=pltpu.PrefetchScalarGridSpec(
+            num_scalar_prefetch=1,
+            grid=(HEADS // step,),
+            in_specs=[
+                pl.BlockSpec((step, HALF, LANES), lambda i, c: (i, LANES // HALF, 0)),
+                pl.BlockSpec((step, HALF, LANES), lambda i, c: (i, 0, 0)),
+            ],
+            out_specs=pl.BlockSpec((LANES, step * LANES), lambda i, c: (0, i)),
+        ),
+        out_shape=jax.ShapeDtypeStruct((LANES, HEADS * LANES), F32),
+        cost_estimate=pl.CostEstimate(flops=0, bytes_accessed=3 << 20, transcendentals=0),
+        compiler_params=pltpu.CompilerParams(vmem_limit_bytes=SMALL),
+        name="join_taps",
+    )(core, last, other)
 
 
 def exchange(packed):
@@ -403,12 +434,18 @@
     grads, grad_mixed = attention(need, packed, recv, mixed)
     grads = exchange(grads)
     last, grad_taps = conv_backward(me, grad_mixed, recv, filter_taps)
-    grad_taps = grad_taps + lax.ppermute(grad_taps, "dp", [(0, 1), (1, 0), (2, 3), (3, 2)])
-    grad_taps = grad_taps + lax.ppermute(grad_taps, "dp", [(0, 2), (2, 0), (1, 3), (3, 1)])
-    shared = jnp.broadcast_to(grad_taps.astype(BF16)[None], (blocks, LANES, LANES))
+    near = [(0, 1), (1, 0), (2, 3), (3, 2)]
+    core = lax.rem(lax.axis_index("dp").astype(jnp.int32), 2)
+    mine = lax.dynamic_slice_in_dim(grad_taps, core * HALF, HALF, 0)
+    theirs = lax.dynamic_slice_in_dim(grad_taps, (1 - core) * HALF, HALF, 0)
+    mine = mine + lax.ppermute(theirs, "dp", near)
+    mine = mine + lax.ppermute(mine, "dp", [(0, 2), (2, 0), (1, 3), (3, 1)])
+    shared = jnp.broadcast_to(mine.astype(BF16)[None], (blocks, HALF, LANES))
     last = exchange(last.at[:, LANES:].set(shared))
+    other = lax.ppermute(last[:, LANES:], "dp", near)
     grad_query, grad_key, grad_gate = unpack(grads, (BF16, BF16, BF16))
-    grad_values, grad_filter = unpack(last, (BF16, F32))
+    (grad_values,) = unpack(last, (BF16,))
+    grad_filter = join_taps(core[None], last, other)
     return grad_query[None], grad_key[None], grad_gate[None], grad_values[None], grad_filter
 
 

time: 224 us -> 218 us (0.973)
  blocking collectives: 36.9 us -> 31.2 us
    all_to_all x1, blocking collectives: 36.9 us -> 31.2 us  [exchange(): return lax.all_to_all(packed, 'ctx', 0, 0, tiled=True)]
    ppermute x2 -> x3, waiting for transfers between devices: 5.24 us -> 5.32 us  [the longest x1 3.42 us: on_device(): mine = mine + lax.ppermute(mine, 'dp', [(0, 2), (2, 0), (1, 3), (3, 1)])]
  transfers between devices with their start and end apart: 5 -> 6, of which waited for: 5 -> 6; matrix products, arithmetic and copies ran while one was open for 0% -> 0% of each run, Pallas kernels for 9% -> 10%
where the time goes in v3:
time: 218 us; the launch traced here: 217 us
  waiting for transfers between devices  93.1 us (43%)
  Pallas kernels  65.9 us (30%)
  blocking collectives  31.2 us (14%)
  starting transfers between devices  22.8 us (10%)
    all_to_all x3, waiting for transfers between devices, exchange(): return lax.all_to_all(packed, 'ctx', 0, 0, tiled=True)  87.7 us
    all_to_all x1, blocking collectives, exchange(): return lax.all_to_all(packed, 'ctx', 0, 0, tiled=True)  31.2 us
    all_to_all x3, starting transfers between devices, exchange(): return lax.all_to_all(packed, 'ctx', 0, 0, tiled=True)  22.2 us
    pallas_call x1, Pallas kernels, conv_backward(): pl.pallas_call(body, grid_spec=pltpu.PrefetchScalarGridSpec(num_scalar_pr...  20.3 us
    pallas_call x1, Pallas kernels, attention(): pl.pallas_call(body, grid_spec=pltpu.PrefetchScalarGridSpec(num_scalar_pr...  19.2 us
    pallas_call x1, Pallas kernels, conv_forward(): pl.pallas_call(body, grid_spec=pltpu.PrefetchScalarGridSpec(num_scalar_pr...  14.2 us
    pallas_call x2, Pallas kernels, pack(): pl.pallas_call(body, grid=(HEADS // step,), in_specs=specs, out_specs=pl....  6.01 us
    pallas_call x2, Pallas kernels, unpack(): pl.pallas_call(body, grid=(HEADS // step,), in_specs=[pl.BlockSpec((step,...  4.67 us
  transfers between devices with their start and end apart: 6, of which 6 were waited for; matrix products, arithmetic and copies ran while one was open for 0% of the time, Pallas kernels for 10%

profile of v3, /device:TPU:6, one launch (start us, length us, event | category | flops | bytes accessed | tf_op | source)
XLA Modules:
  0.0 217.0 jit_solution(5124979425682755113)
XLA Ops:
  0.6 2.1 pack.2
  2.8 10.9 %all-to-all-start = ((bf16[32,136,128]{2,1,0:T(8,128)(2,1)}), bf16[32,136,128]{2,1,0:T(8,128)(2,1)S(1)}, u32[]{:S(2)}, u32[]{:S(2)}) async-start(bf16[32,136,128]{2,1,0:T(8,128)(2,1)} %pack.2), calls=%async_computation | async-start | bytes 2228224 | tf_op jit(solution)/shard_map/all_to_all | solution.py:421
  13.7 3.9 %pack.3 = bf16[32,512,128]{2,1,0:T(8,128)(2,1)} custom-call(bf16[128,4096]{1,0:T(8,128)(2,1)} %bitcast.16, bf16[128,4096]{1,0:T(8,128)(2,1)} %bitcast.17, bf16[128,4096]{1,0:T(8,128)(2,1)} %bitcast.18, bf16[128,4096]{1,0:T(8,128)(2,1)} %bitcast.19), custom_call_target="tpu_custom_call" | custom-call | bytes 8388608 | tf_op jit(solution)/shard_map/pack/pallas_call | solution.py:50
  17.5 14.3 %all-to-all-done.v_ref.info_ref = bf16[32,136,128]{2,1,0:T(8,128)(2,1)S(1)} async-done(((bf16[32,136,128]{2,1,0:T(8,128)(2,1)}), bf16[32,136,128]{2,1,0:T(8,128)(2,1)S(1)}, u32[]{:S(2)}, u32[]{:S(2)}) %all-to-all-start) | async-done | bytes 1114144 | tf_op jit(solution)/shard_map/all_to_all | solution.py:421
  31.8 0.0 copy-start
  31.8 5.4 %all-to-all-start.1 = ((bf16[32,512,128]{2,1,0:T(8,128)(2,1)}), bf16[32,512,128]{2,1,0:T(8,128)(2,1)}, u32[]{:S(2)}, u32[]{:S(2)}) async-start(bf16[32,512,128]{2,1,0:T(8,128)(2,1)} %pack.3), calls=%async_computation.1 | async-start | bytes 8388608 | tf_op jit(solution)/shard_map/all_to_all | solution.py:421
  37.3 0.0 copy-done
  37.3 0.1 copy.13
  37.4 0.1 slice.40
  37.5 14.2 %conv_forward.1.mixed_hbm = f32[32,128,128]{2,1,0:T(8,128)} custom-call(s32[1]{0:T(128)} %bitcast.7.me_ref, bf16[32,136,128]{2,1,0:T(8,128)(2,1)} %copy-done, f32[128,4096]{1,0:T(8,128)} %taps_ref.3), custom_call_target="tpu_custom_call" | custom-call | flops 2147483648 | bytes 4194304 | tf_op jit(solution)/shard_map/conv_forward/pallas_call | solution.py:132
  51.7 0.5 fusion.need_ref
  52.2 37.5 %all-to-all-done.1.packed_ref = bf16[32,512,128]{2,1,0:T(8,128)(2,1)} async-done(((bf16[32,512,128]{2,1,0:T(8,128)(2,1)}), bf16[32,512,128]{2,1,0:T(8,128)(2,1)}, u32[]{:S(2)}, u32[]{:S(2)}) %all-to-all-start.1) | async-done | bytes 4194336 | tf_op jit(solution)/shard_map/all_to_all | solution.py:421
  89.7 19.2 %attention.1 = (bf16[32,384,128]{2,1,0:T(8,128)(2,1)}, bf16[32,128,128]{2,1,0:T(8,128)(2,1)}) custom-call(s32[16]{0:T(128)} %fusion.need_ref, bf16[32,512,128]{2,1,0:T(8,128)(2,1)} %all-to-all-done.1.packed_ref, bf16[32,136,128]{2,1,0:T(8,128)(2,1)} %copy-done, f32[32,128,128]{2,1,0:T(8,128)} %conv_forward.1.mixed_hbm), custom_call_target="tpu_custom_call" | custom-call | flops 4697620480 | bytes 10485760 | tf_op jit(solution)/shard_map/attention/pallas_call | solution.py:273
  108.9 20.3 %conv_backward.1 = (bf16[32,192,128]{2,1,0:T(8,128)(2,1)}, f32[128,128]{1,0:T(8,128)}) custom-call(s32[1]{0:T(128)} %bitcast.7.me_ref, bf16[32,128,128]{2,1,0:T(8,128)(2,1)} %get-tuple-element.28.gm_ref, bf16[32,136,128]{2,1,0:T(8,128)(2,1)} %copy-done, f32[128,4096]{1,0:T(8,128)} %taps_ref.3), custom_call_target="tpu_custom_call" | custom-call | flops 2147483648 | bytes 4194304 | tf_op jit(solution)/shard_map/conv_backward/pallas_call | solution.py:357
  129.2 0.8 constant_dynamic-slice_fusion
  130.0 0.0 collective-permute-start
  130.0 1.2 collective-permute-done
  131.2 0.8 dynamic-slice_add_fusion
  132.0 0.5 collective-permute-start.1
  132.5 3.4 %collective-permute-done.1 = f32[64,128]{1,0:T(8,128)S(1)} collective-permute-done((f32[64,128]{1,0:T(8,128)S(1)}, f32[64,128]{1,0:T(8,128)S(1)}, u32[]{:S(2)}, u32[]{:S(2)}) %collective-permute-start.1) | collective-permute-done | bytes 32800 | tf_op jit(solution)/shard_map/ppermute | solution.py:442
  135.9 0.9 broadcast_dynamic-update-slice_fusion
  136.8 31.2 %all_to_all.20.refs_0_.mine_ref = bf16[32,192,128]{2,1,0:T(8,128)(2,1)S(1)} all-to-all(bf16[32,192,128]{2,1,0:T(8,128)(2,1)} %broadcast_dynamic-update-slice_fusion), channel_id=1, replica_groups=mesh['dp'=4,'ctx'=32] {'ctx'}, dimensions={0} | all-to-all | bytes 3145728 | tf_op jit(solution)/shard_map/all_to_all | solution.py:421
  168.0 6.0 %all-to-all-start.2 = ((bf16[32,384,128]{2,1,0:T(8,128)(2,1)}), bf16[32,384,128]{2,1,0:T(8,128)(2,1)}, u32[]{:S(2)}, u32[]{:S(2)}) async-start(bf16[32,384,128]{2,1,0:T(8,128)(2,1)} %get-tuple-element.24), calls=%async_computation.2 | async-start | bytes 6291456 | tf_op jit(solution)/shard_map/all_to_all | solution.py:421
  174.0 0.1 collective-permute-start.2
  174.1 1.2 unpack.3
  175.3 0.7 collective-permute-done.2.other_ref
  176.0 1.5 join_taps.1
  177.5 36.0 %all-to-all-done.2.refs_0_ = bf16[32,384,128]{2,1,0:T(8,128)(2,1)} async-done(((bf16[32,384,128]{2,1,0:T(8,128)(2,1)}), bf16[32,384,128]{2,1,0:T(8,128)(2,1)}, u32[]{:S(2)}, u32[]{:S(2)}) %all-to-all-start.2) | async-done | bytes 3145760 | tf_op jit(solution)/shard_map/all_to_all | solution.py:421
  213.5 3.5 %unpack.2 = (bf16[128,4096]{1,0:T(8,128)(2,1)}, bf16[128,4096]{1,0:T(8,128)(2,1)}, bf16[128,4096]{1,0:T(8,128)(2,1)}) custom-call(bf16[32,384,128]{2,1,0:T(8,128)(2,1)} %all-to-all-done.2.refs_0_), custom_call_target="tpu_custom_call" | custom-call | bytes 6291456 | tf_op jit(solution)/shard_map/unpack/pallas_call | solution.py:71
  (4 shorter events, 0.1 us)
Async XLA Ops:
  2.8 29.1 %all-to-all-start = ((bf16[32,136,128]{2,1,0:T(8,128)(2,1)}), bf16[32,136,128]{2,1,0:T(8,128)(2,1)S(1)}, u32[]{:S(2)}, u32[]{:S(2)}) async-start(bf16[32,136,128]{2,1,0:T(8,128)(2,1)} %pack.2), calls=%async_computation | async-start | bytes 2228224 | tf_op jit(solution)/shard_map/all_to_all | solution.py:421
  31.8 5.4 %copy-start = (bf16[32,136,128]{2,1,0:T(8,128)(2,1)}, bf16[32,136,128]{2,1,0:T(8,128)(2,1)S(1)}, u32[]{:S(2)}) copy-start(bf16[32,136,128]{2,1,0:T(8,128)(2,1)S(1)} %all-to-all-done.v_ref.info_ref) | copy-start | bytes 3342340
  31.8 57.9 %all-to-all-start.1 = ((bf16[32,512,128]{2,1,0:T(8,128)(2,1)}), bf16[32,512,128]{2,1,0:T(8,128)(2,1)}, u32[]{:S(2)}, u32[]{:S(2)}) async-start(bf16[32,512,128]{2,1,0:T(8,128)(2,1)} %pack.3), calls=%async_computation.1 | async-start | bytes 8388608 | tf_op jit(solution)/shard_map/all_to_all | solution.py:421
  130.0 1.2 collective-permute-start
  132.0 3.9 %collective-permute-start.1 = (f32[64,128]{1,0:T(8,128)S(1)}, f32[64,128]{1,0:T(8,128)S(1)}, u32[]{:S(2)}, u32[]{:S(2)}) collective-permute-start(f32[64,128]{1,0:T(8,128)S(1)} %dynamic-slice_add_fusion), channel_id=1, source_target_pairs={{0,64},{64,0},{32,96},{96,32},{1,65},{65,1},{33,97},{97,33},{2,66}... | collective-permute-start | bytes 98312 | tf_op jit(solution)/shard_map/ppermute | solution.py:442
  168.0 45.5 %all-to-all-start.2 = ((bf16[32,384,128]{2,1,0:T(8,128)(2,1)}), bf16[32,384,128]{2,1,0:T(8,128)(2,1)}, u32[]{:S(2)}, u32[]{:S(2)}) async-start(bf16[32,384,128]{2,1,0:T(8,128)(2,1)} %get-tuple-element.24), calls=%async_computation.2 | async-start | bytes 6291456 | tf_op jit(solution)/shard_map/all_to_all | solution.py:421
  174.0 2.0 collective-permute-start.2

commit v4 on v3

--- a/solution.py
+++ b/solution.py
@@ -154,6 +154,8 @@
 
 
 CHUNK = 8
+AHEAD = 1
+EVERY = 1
 FLUSH = TWIN * QT
 
 
@@ -186,9 +188,12 @@
                 pltpu.make_async_copy(gm_ref.at[at], gm_hbm.at[at], out_sem.at[f, 1]),
             ]
 
-        for c in range(chunks):
+        def request(c):
             for move in arrivals(c):
                 move.start()
+
+        for c in range(AHEAD):
+            request(c)
         ks[0:pad, :] = jnp.zeros((pad, LANES), BF16)
         hs[0:pad, :] = jnp.zeros((pad, LANES), BF16)
         kt[:, 0:pad] = jnp.zeros((LANES, pad), BF16)
@@ -201,6 +206,7 @@
         def prepare(c):
             for move in arrivals(c):
                 move.wait()
+            pl.when(c + AHEAD < chunks)(lambda: request(c + AHEAD))
             for u in range(CHUNK):
                 b = c * CHUNK + u
                 at = pl.multiple_of(pad + b * LANES, LANES)
@@ -220,11 +226,65 @@
             for move in departures(f):
                 move.start()
 
+        def head(start, s, dp, window, result):
+            below = lax.broadcasted_iota(jnp.int32, (LANES, LANES), 0) <= lax.broadcasted_iota(
+                jnp.int32, (LANES, LANES), 1
+            )
+            kpos = lax.broadcasted_iota(jnp.int32, (LANES, LANES), 0)
+            halves, grads = [], []
+            for j in range(QT):
+                count = window - (QT - 1 - j)
+                lanes = slice(j * LANES, (j + 1) * LANES)
+                scores, weights, probs, half, replies = [], [], [], [], []
+                top = None
+                for b in range(count):
+                    score = jnp.where(
+                        kpos >= start[:, lanes] - b * LANES, s[b * LANES : (b + 1) * LANES, lanes], -1e30
+                    )
+                    if b == count - 1:
+                        score = jnp.where(below, score, -1e30)
+                    scores.append(score)
+                    most = jnp.max(score, 0, keepdims=True)
+                    top = most if top is None else jnp.maximum(top, most)
+                    yield
+                top = top * factor
+                total = 0.0
+                for b in range(count):
+                    weights.append(jnp.exp2(scores[b] * factor - top))
+                    total = total + jnp.sum(weights[b], 0, keepdims=True)
+                    yield
+                share = 1.0 / total
+                delta = 0.0
+                for b in range(count):
+                    probs.append(weights[b] * share)
+                    half.append(probs[b].astype(BF16))
+                    replies.append(dp[b * LANES : (b + 1) * LANES, lanes])
+                    delta = delta + jnp.sum(half[b].astype(F32) * replies[b], 0, keepdims=True)
+                    yield
+                grad = []
+                for b in range(count):
+                    grad.append((probs[b] * (replies[b] - delta)).astype(BF16))
+                    yield
+                gap = [jnp.zeros((LANES, LANES), BF16)] * (window - count)
+                halves.append(jnp.concatenate(half + gap, 0))
+                grads.append(jnp.concatenate(grad + gap, 0))
+            result.append(jnp.concatenate(halves, 1))
+            result.append(jnp.concatenate(grads, 1))
+
+        def tail(i, first, q, d, window, result):
+            half, ds = result
+            span = window * LANES
+            dq = jnp.dot(kt[:, pl.ds(first, span)], ds, preferred_element_type=F32) * scale
+            for j in range(QT):
+                out_ref[QT * i + j, 0:LANES] = dq[:, j * LANES : (j + 1) * LANES].T.astype(BF16)
+            yield
+            for acc, left, right in ((dv, half, d), (dk, ds, q)):
+                acc[pl.ds(first, span), :] += jnp.dot(left, right, preferred_element_type=F32)
+                yield
+
         def tiles_of(g, window):
             span = window * LANES
-            kpos = lax.broadcasted_iota(jnp.int32, (span, width), 0)
-            qpos = lax.broadcasted_iota(jnp.int32, (span, width), 1) + (window - QT) * LANES
-            held = []
+            before = iter(())
             for u in range(TWIN):
                 i = TWIN * g + u
                 first = pl.multiple_of((QT * i + QT - window) * LANES + pad, LANES)
@@ -232,22 +292,16 @@
                 d = d_ref[pl.ds(QT * i, QT)].reshape(width, LANES)
                 start = st[i, 0:1, :].astype(jnp.int32) - (first - pad)
                 s = contract(ks[pl.ds(first, span), :], q, 1, 1)
-                s = jnp.where((kpos >= start) & (kpos <= qpos), s, -1e30)
-                top = jnp.max(s, 0, keepdims=True) * factor
-                p = jnp.exp2(s * factor - top)
-                p = p * (1.0 / jnp.sum(p, 0, keepdims=True))
-                half = p.astype(BF16)
                 dp = contract(hs[pl.ds(first, span), :], d, 1, 1)
-                delta = jnp.sum(half.astype(F32) * dp, 0, keepdims=True)
-                ds = (p * (dp - delta)).astype(BF16)
-                held.append((i, first, q, d, half, ds))
-            for i, first, q, d, half, ds in held:
-                dq = jnp.dot(kt[:, pl.ds(first, span)], ds, preferred_element_type=F32) * scale
-                for j in range(QT):
-                    out_ref[QT * i + j, 0:LANES] = dq[:, j * LANES : (j + 1) * LANES].T.astype(BF16)
-            for i, first, q, d, half, ds in held:
-                dv[pl.ds(first, span), :] += jnp.dot(half, d, preferred_element_type=F32)
-                dk[pl.ds(first, span), :] += jnp.dot(ds, q, preferred_element_type=F32)
+                result = []
+                for at, _ in enumerate(head(start, s, dp, window, result)):
+                    if at % (EVERY * window) == 0:
+                        next(before, None)
+                for _ in before:
+                    pass
+                before = tail(i, first, q, d, window, result)
+            for _ in before:
+                pass
 
         def step(g, carry):
             pl.when(g % (CHUNK // FLUSH) == 0)(lambda: prepare(g // (CHUNK // FLUSH)))

time: 218 us -> 216 us (level)
  no operation moved by 1% of the time
where the time goes in v4:
time: 216 us
  waiting for transfers between devices  92.9 us (43%)
  Pallas kernels  64.5 us (30%)
  blocking collectives  31.2 us (14%)
  starting transfers between devices  22.9 us (11%)
    all_to_all x3, waiting for transfers between devices, exchange(): return lax.all_to_all(packed, 'ctx', 0, 0, tiled=True)  87.7 us
    all_to_all x1, blocking collectives, exchange(): return lax.all_to_all(packed, 'ctx', 0, 0, tiled=True)  31.2 us
    all_to_all x3, starting transfers between devices, exchange(): return lax.all_to_all(packed, 'ctx', 0, 0, tiled=True)  22.2 us
    pallas_call x1, Pallas kernels, conv_backward(): pl.pallas_call(body, grid_spec=pltpu.PrefetchScalarGridSpec(num_scalar_pr...  20.3 us
    pallas_call x1, Pallas kernels, attention(): pl.pallas_call(body, grid_spec=pltpu.PrefetchScalarGridSpec(num_scalar_pr...  17.8 us
    pallas_call x1, Pallas kernels, conv_forward(): pl.pallas_call(body, grid_spec=pltpu.PrefetchScalarGridSpec(num_scalar_pr...  14.2 us
    pallas_call x2, Pallas kernels, pack(): pl.pallas_call(body, grid=(HEADS // step,), in_specs=specs, out_specs=pl....  6.01 us
    pallas_call x2, Pallas kernels, unpack(): pl.pallas_call(body, grid=(HEADS // step,), in_specs=[pl.BlockSpec((step,...  4.67 us
  transfers between devices with their start and end apart: 6, of which 6 were waited for; matrix products, arithmetic and copies ran while one was open for 0% of the time, Pallas kernels for 10%

profile of v4, /device:TPU:6, one launch (start us, length us, event | category | flops | bytes accessed | tf_op | source)
XLA Modules:
  0.0 215.5 jit_solution(17086787953488287321)
XLA Ops:
  0.6 2.1 pack.2
  2.8 10.9 %all-to-all-start = ((bf16[32,136,128]{2,1,0:T(8,128)(2,1)}), bf16[32,136,128]{2,1,0:T(8,128)(2,1)S(1)}, u32[]{:S(2)}, u32[]{:S(2)}) async-start(bf16[32,136,128]{2,1,0:T(8,128)(2,1)} %pack.2), calls=%async_computation | async-start | bytes 2228224 | tf_op jit(solution)/shard_map/all_to_all | solution.py:475
  13.7 3.9 %pack.3 = bf16[32,512,128]{2,1,0:T(8,128)(2,1)} custom-call(bf16[128,4096]{1,0:T(8,128)(2,1)} %bitcast.16, bf16[128,4096]{1,0:T(8,128)(2,1)} %bitcast.17, bf16[128,4096]{1,0:T(8,128)(2,1)} %bitcast.18, bf16[128,4096]{1,0:T(8,128)(2,1)} %bitcast.19), custom_call_target="tpu_custom_call" | custom-call | bytes 8388608 | tf_op jit(solution)/shard_map/pack/pallas_call | solution.py:50
  17.5 14.3 %all-to-all-done.v_ref.info_ref = bf16[32,136,128]{2,1,0:T(8,128)(2,1)S(1)} async-done(((bf16[32,136,128]{2,1,0:T(8,128)(2,1)}), bf16[32,136,128]{2,1,0:T(8,128)(2,1)S(1)}, u32[]{:S(2)}, u32[]{:S(2)}) %all-to-all-start) | async-done | bytes 1114144 | tf_op jit(solution)/shard_map/all_to_all | solution.py:475
  31.8 0.0 copy-start
  31.8 5.4 %all-to-all-start.1 = ((bf16[32,512,128]{2,1,0:T(8,128)(2,1)}), bf16[32,512,128]{2,1,0:T(8,128)(2,1)}, u32[]{:S(2)}, u32[]{:S(2)}) async-start(bf16[32,512,128]{2,1,0:T(8,128)(2,1)} %pack.3), calls=%async_computation.1 | async-start | bytes 8388608 | tf_op jit(solution)/shard_map/all_to_all | solution.py:475
  37.3 0.0 copy-done
  37.3 0.1 copy.13
  37.4 0.1 slice.40
  37.5 14.2 %conv_forward.1.mixed_hbm = f32[32,128,128]{2,1,0:T(8,128)} custom-call(s32[1]{0:T(128)} %bitcast.7.me_ref, bf16[32,136,128]{2,1,0:T(8,128)(2,1)} %copy-done, f32[128,4096]{1,0:T(8,128)} %taps_ref.3), custom_call_target="tpu_custom_call" | custom-call | flops 2147483648 | bytes 4194304 | tf_op jit(solution)/shard_map/conv_forward/pallas_call | solution.py:132
  51.7 0.5 fusion.need_ref
  52.2 37.5 %all-to-all-done.1.packed_ref = bf16[32,512,128]{2,1,0:T(8,128)(2,1)} async-done(((bf16[32,512,128]{2,1,0:T(8,128)(2,1)}), bf16[32,512,128]{2,1,0:T(8,128)(2,1)}, u32[]{:S(2)}, u32[]{:S(2)}) %all-to-all-start.1) | async-done | bytes 4194336 | tf_op jit(solution)/shard_map/all_to_all | solution.py:475
  89.7 17.8 %attention.1 = (bf16[32,384,128]{2,1,0:T(8,128)(2,1)}, bf16[32,128,128]{2,1,0:T(8,128)(2,1)}) custom-call(s32[16]{0:T(128)} %fusion.need_ref, bf16[32,512,128]{2,1,0:T(8,128)(2,1)} %all-to-all-done.1.packed_ref, bf16[32,136,128]{2,1,0:T(8,128)(2,1)} %copy-done, f32[32,128,128]{2,1,0:T(8,128)} %conv_forward.1.mixed_hbm), custom_call_target="tpu_custom_call" | custom-call | flops 4697620480 | bytes 10485760 | tf_op jit(solution)/shard_map/attention/pallas_call | solution.py:327
  107.5 20.3 %conv_backward.1 = (bf16[32,192,128]{2,1,0:T(8,128)(2,1)}, f32[128,128]{1,0:T(8,128)}) custom-call(s32[1]{0:T(128)} %bitcast.7.me_ref, bf16[32,128,128]{2,1,0:T(8,128)(2,1)} %get-tuple-element.28.gm_ref, bf16[32,136,128]{2,1,0:T(8,128)(2,1)} %copy-done, f32[128,4096]{1,0:T(8,128)} %taps_ref.3), custom_call_target="tpu_custom_call" | custom-call | flops 2147483648 | bytes 4194304 | tf_op jit(solution)/shard_map/conv_backward/pallas_call | solution.py:411
  127.8 0.8 constant_dynamic-slice_fusion
  128.6 0.0 collective-permute-start
  128.6 1.2 collective-permute-done
  129.8 0.8 dynamic-slice_add_fusion
  130.5 0.6 collective-permute-start.1
  131.1 3.3 %collective-permute-done.1 = f32[64,128]{1,0:T(8,128)S(1)} collective-permute-done((f32[64,128]{1,0:T(8,128)S(1)}, f32[64,128]{1,0:T(8,128)S(1)}, u32[]{:S(2)}, u32[]{:S(2)}) %collective-permute-start.1) | collective-permute-done | bytes 32800 | tf_op jit(solution)/shard_map/ppermute | solution.py:496
  134.5 0.9 broadcast_dynamic-update-slice_fusion
  135.4 31.2 %all_to_all.20.refs_0_.mine_ref = bf16[32,192,128]{2,1,0:T(8,128)(2,1)S(1)} all-to-all(bf16[32,192,128]{2,1,0:T(8,128)(2,1)} %broadcast_dynamic-update-slice_fusion), channel_id=1, replica_groups=mesh['dp'=4,'ctx'=32] {'ctx'}, dimensions={0} | all-to-all | bytes 3145728 | tf_op jit(solution)/shard_map/all_to_all | solution.py:475
  166.6 6.0 %all-to-all-start.2 = ((bf16[32,384,128]{2,1,0:T(8,128)(2,1)}), bf16[32,384,128]{2,1,0:T(8,128)(2,1)}, u32[]{:S(2)}, u32[]{:S(2)}) async-start(bf16[32,384,128]{2,1,0:T(8,128)(2,1)} %get-tuple-element.24), calls=%async_computation.2 | async-start | bytes 6291456 | tf_op jit(solution)/shard_map/all_to_all | solution.py:475
  172.6 0.1 collective-permute-start.2
  172.7 1.2 unpack.3
  173.9 0.7 collective-permute-done.2.other_ref
  174.6 1.5 join_taps.1
  176.1 36.0 %all-to-all-done.2.refs_0_ = bf16[32,384,128]{2,1,0:T(8,128)(2,1)} async-done(((bf16[32,384,128]{2,1,0:T(8,128)(2,1)}), bf16[32,384,128]{2,1,0:T(8,128)(2,1)}, u32[]{:S(2)}, u32[]{:S(2)}) %all-to-all-start.2) | async-done | bytes 3145760 | tf_op jit(solution)/shard_map/all_to_all | solution.py:475
  212.0 3.5 %unpack.2 = (bf16[128,4096]{1,0:T(8,128)(2,1)}, bf16[128,4096]{1,0:T(8,128)(2,1)}, bf16[128,4096]{1,0:T(8,128)(2,1)}) custom-call(bf16[32,384,128]{2,1,0:T(8,128)(2,1)} %all-to-all-done.2.refs_0_), custom_call_target="tpu_custom_call" | custom-call | bytes 6291456 | tf_op jit(solution)/shard_map/unpack/pallas_call | solution.py:71
  (4 shorter events, 0.1 us)
Async XLA Ops:
  2.8 29.1 %all-to-all-start = ((bf16[32,136,128]{2,1,0:T(8,128)(2,1)}), bf16[32,136,128]{2,1,0:T(8,128)(2,1)S(1)}, u32[]{:S(2)}, u32[]{:S(2)}) async-start(bf16[32,136,128]{2,1,0:T(8,128)(2,1)} %pack.2), calls=%async_computation | async-start | bytes 2228224 | tf_op jit(solution)/shard_map/all_to_all | solution.py:475
  31.8 5.4 %copy-start = (bf16[32,136,128]{2,1,0:T(8,128)(2,1)}, bf16[32,136,128]{2,1,0:T(8,128)(2,1)S(1)}, u32[]{:S(2)}) copy-start(bf16[32,136,128]{2,1,0:T(8,128)(2,1)S(1)} %all-to-all-done.v_ref.info_ref) | copy-start | bytes 3342340
  31.8 57.9 %all-to-all-start.1 = ((bf16[32,512,128]{2,1,0:T(8,128)(2,1)}), bf16[32,512,128]{2,1,0:T(8,128)(2,1)}, u32[]{:S(2)}, u32[]{:S(2)}) async-start(bf16[32,512,128]{2,1,0:T(8,128)(2,1)} %pack.3), calls=%async_computation.1 | async-start | bytes 8388608 | tf_op jit(solution)/shard_map/all_to_all | solution.py:475
  128.6 1.2 collective-permute-start
  130.5 3.9 %collective-permute-start.1 = (f32[64,128]{1,0:T(8,128)S(1)}, f32[64,128]{1,0:T(8,128)S(1)}, u32[]{:S(2)}, u32[]{:S(2)}) collective-permute-start(f32[64,128]{1,0:T(8,128)S(1)} %dynamic-slice_add_fusion), channel_id=1, source_target_pairs={{0,64},{64,0},{32,96},{96,32},{1,65},{65,1},{33,97},{97,33},{2,66}... | collective-permute-start | bytes 98312 | tf_op jit(solution)/shard_map/ppermute | solution.py:496
  166.6 45.5 %all-to-all-start.2 = ((bf16[32,384,128]{2,1,0:T(8,128)(2,1)}), bf16[32,384,128]{2,1,0:T(8,128)(2,1)}, u32[]{:S(2)}, u32[]{:S(2)}) async-start(bf16[32,384,128]{2,1,0:T(8,128)(2,1)} %get-tuple-element.24), calls=%async_computation.2 | async-start | bytes 6291456 | tf_op jit(solution)/shard_map/all_to_all | solution.py:475
  172.6 2.0 collective-permute-start.2

commit v5 on v4

--- a/solution.py
+++ b/solution.py
@@ -284,18 +284,28 @@
 
         def tiles_of(g, window):
             span = window * LANES
-            before = iter(())
-            for u in range(TWIN):
+            ready = []
+
+            def scores_of(u):
                 i = TWIN * g + u
                 first = pl.multiple_of((QT * i + QT - window) * LANES + pad, LANES)
                 q = q_ref[pl.ds(QT * i, QT)].reshape(width, LANES)
                 d = d_ref[pl.ds(QT * i, QT)].reshape(width, LANES)
+                s = contract(ks[pl.ds(first, span), :], q, 1, 1)
+                yield
+                dp = contract(hs[pl.ds(first, span), :], d, 1, 1)
+                ready.append((i, first, q, d, s, dp))
+                yield
+
+            for _ in scores_of(0):
+                pass
+            before = scores_of(1)
+            for u in range(TWIN):
+                i, first, q, d, s, dp = ready[u]
                 start = st[i, 0:1, :].astype(jnp.int32) - (first - pad)
-                s = contract(ks[pl.ds(first, span), :], q, 1, 1)
-                dp = contract(hs[pl.ds(first, span), :], d, 1, 1)
                 result = []
                 for at, _ in enumerate(head(start, s, dp, window, result)):
-                    if at % (EVERY * window) == 0:
+                    if at % (EVERY * window) == window // 2:
                         next(before, None)
                 for _ in before:
                     pass

time: 216 us -> 216 us (level)
  no operation moved by 1% of the time
where the time goes in v5:
time: 216 us
  waiting for transfers between devices  92.9 us (43%)
  Pallas kernels  64.5 us (30%)
  blocking collectives  31.2 us (14%)
  starting transfers between devices  22.9 us (11%)
    all_to_all x3, waiting for transfers between devices, exchange(): return lax.all_to_all(packed, 'ctx', 0, 0, tiled=True)  87.7 us
    all_to_all x1, blocking collectives, exchange(): return lax.all_to_all(packed, 'ctx', 0, 0, tiled=True)  31.2 us
    all_to_all x3, starting transfers between devices, exchange(): return lax.all_to_all(packed, 'ctx', 0, 0, tiled=True)  22.2 us
    pallas_call x1, Pallas kernels, conv_backward(): pl.pallas_call(body, grid_spec=pltpu.PrefetchScalarGridSpec(num_scalar_pr...  20.3 us
    pallas_call x1, Pallas kernels, attention(): pl.pallas_call(body, grid_spec=pltpu.PrefetchScalarGridSpec(num_scalar_pr...  17.8 us
    pallas_call x1, Pallas kernels, conv_forward(): pl.pallas_call(body, grid_spec=pltpu.PrefetchScalarGridSpec(num_scalar_pr...  14.2 us
    pallas_call x2, Pallas kernels, pack(): pl.pallas_call(body, grid=(HEADS // step,), in_specs=specs, out_specs=pl....  6.01 us
    pallas_call x2, Pallas kernels, unpack(): pl.pallas_call(body, grid=(HEADS // step,), in_specs=[pl.BlockSpec((step,...  4.67 us
  transfers between devices with their start and end apart: 6, of which 6 were waited for; matrix products, arithmetic and copies ran while one was open for 0% of the time, Pallas kernels for 10%

profile of v5, /device:TPU:6, one launch (start us, length us, event | category | flops | bytes accessed | tf_op | source)
XLA Modules:
  0.0 215.5 jit_solution(1237801794985195852)
XLA Ops:
  0.6 2.1 pack.2
  2.8 10.9 %all-to-all-start = ((bf16[32,136,128]{2,1,0:T(8,128)(2,1)}), bf16[32,136,128]{2,1,0:T(8,128)(2,1)S(1)}, u32[]{:S(2)}, u32[]{:S(2)}) async-start(bf16[32,136,128]{2,1,0:T(8,128)(2,1)} %pack.2), calls=%async_computation | async-start | bytes 2228224 | tf_op jit(solution)/shard_map/all_to_all | solution.py:485
  13.7 3.9 %pack.3 = bf16[32,512,128]{2,1,0:T(8,128)(2,1)} custom-call(bf16[128,4096]{1,0:T(8,128)(2,1)} %bitcast.16, bf16[128,4096]{1,0:T(8,128)(2,1)} %bitcast.17, bf16[128,4096]{1,0:T(8,128)(2,1)} %bitcast.18, bf16[128,4096]{1,0:T(8,128)(2,1)} %bitcast.19), custom_call_target="tpu_custom_call" | custom-call | bytes 8388608 | tf_op jit(solution)/shard_map/pack/pallas_call | solution.py:50
  17.5 14.3 %all-to-all-done.v_ref.info_ref = bf16[32,136,128]{2,1,0:T(8,128)(2,1)S(1)} async-done(((bf16[32,136,128]{2,1,0:T(8,128)(2,1)}), bf16[32,136,128]{2,1,0:T(8,128)(2,1)S(1)}, u32[]{:S(2)}, u32[]{:S(2)}) %all-to-all-start) | async-done | bytes 1114144 | tf_op jit(solution)/shard_map/all_to_all | solution.py:485
  31.8 0.0 copy-start
  31.8 5.4 %all-to-all-start.1 = ((bf16[32,512,128]{2,1,0:T(8,128)(2,1)}), bf16[32,512,128]{2,1,0:T(8,128)(2,1)}, u32[]{:S(2)}, u32[]{:S(2)}) async-start(bf16[32,512,128]{2,1,0:T(8,128)(2,1)} %pack.3), calls=%async_computation.1 | async-start | bytes 8388608 | tf_op jit(solution)/shard_map/all_to_all | solution.py:485
  37.3 0.0 copy-done
  37.3 0.1 copy.13
  37.4 0.1 slice.40
  37.5 14.2 %conv_forward.1.mixed_hbm = f32[32,128,128]{2,1,0:T(8,128)} custom-call(s32[1]{0:T(128)} %bitcast.7.me_ref, bf16[32,136,128]{2,1,0:T(8,128)(2,1)} %copy-done, f32[128,4096]{1,0:T(8,128)} %taps_ref.3), custom_call_target="tpu_custom_call" | custom-call | flops 2147483648 | bytes 4194304 | tf_op jit(solution)/shard_map/conv_forward/pallas_call | solution.py:132
  51.7 0.5 fusion.need_ref
  52.2 37.5 %all-to-all-done.1.packed_ref = bf16[32,512,128]{2,1,0:T(8,128)(2,1)} async-done(((bf16[32,512,128]{2,1,0:T(8,128)(2,1)}), bf16[32,512,128]{2,1,0:T(8,128)(2,1)}, u32[]{:S(2)}, u32[]{:S(2)}) %all-to-all-start.1) | async-done | bytes 4194336 | tf_op jit(solution)/shard_map/all_to_all | solution.py:485
  89.7 17.8 %attention.1 = (bf16[32,384,128]{2,1,0:T(8,128)(2,1)}, bf16[32,128,128]{2,1,0:T(8,128)(2,1)}) custom-call(s32[16]{0:T(128)} %fusion.need_ref, bf16[32,512,128]{2,1,0:T(8,128)(2,1)} %all-to-all-done.1.packed_ref, bf16[32,136,128]{2,1,0:T(8,128)(2,1)} %copy-done, f32[32,128,128]{2,1,0:T(8,128)} %conv_forward.1.mixed_hbm), custom_call_target="tpu_custom_call" | custom-call | flops 4697620480 | bytes 10485760 | tf_op jit(solution)/shard_map/attention/pallas_call | solution.py:337
  107.5 20.3 %conv_backward.1 = (bf16[32,192,128]{2,1,0:T(8,128)(2,1)}, f32[128,128]{1,0:T(8,128)}) custom-call(s32[1]{0:T(128)} %bitcast.7.me_ref, bf16[32,128,128]{2,1,0:T(8,128)(2,1)} %get-tuple-element.28.gm_ref, bf16[32,136,128]{2,1,0:T(8,128)(2,1)} %copy-done, f32[128,4096]{1,0:T(8,128)} %taps_ref.3), custom_call_target="tpu_custom_call" | custom-call | flops 2147483648 | bytes 4194304 | tf_op jit(solution)/shard_map/conv_backward/pallas_call | solution.py:421
  127.8 0.8 constant_dynamic-slice_fusion
  128.6 0.0 collective-permute-start
  128.6 1.2 collective-permute-done
  129.8 0.8 dynamic-slice_add_fusion
  130.5 0.6 collective-permute-start.1
  131.1 3.3 %collective-permute-done.1 = f32[64,128]{1,0:T(8,128)S(1)} collective-permute-done((f32[64,128]{1,0:T(8,128)S(1)}, f32[64,128]{1,0:T(8,128)S(1)}, u32[]{:S(2)}, u32[]{:S(2)}) %collective-permute-start.1) | collective-permute-done | bytes 32800 | tf_op jit(solution)/shard_map/ppermute | solution.py:506
  134.5 0.9 broadcast_dynamic-update-slice_fusion
  135.4 31.2 %all_to_all.20.refs_0_.mine_ref = bf16[32,192,128]{2,1,0:T(8,128)(2,1)S(1)} all-to-all(bf16[32,192,128]{2,1,0:T(8,128)(2,1)} %broadcast_dynamic-update-slice_fusion), channel_id=1, replica_groups=mesh['dp'=4,'ctx'=32] {'ctx'}, dimensions={0} | all-to-all | bytes 3145728 | tf_op jit(solution)/shard_map/all_to_all | solution.py:485
  166.6 6.0 %all-to-all-start.2 = ((bf16[32,384,128]{2,1,0:T(8,128)(2,1)}), bf16[32,384,128]{2,1,0:T(8,128)(2,1)}, u32[]{:S(2)}, u32[]{:S(2)}) async-start(bf16[32,384,128]{2,1,0:T(8,128)(2,1)} %get-tuple-element.24), calls=%async_computation.2 | async-start | bytes 6291456 | tf_op jit(solution)/shard_map/all_to_all | solution.py:485
  172.6 0.1 collective-permute-start.2
  172.7 1.2 unpack.3
  173.9 0.7 collective-permute-done.2.other_ref
  174.6 1.5 join_taps.1
  176.1 36.0 %all-to-all-done.2.refs_0_ = bf16[32,384,128]{2,1,0:T(8,128)(2,1)} async-done(((bf16[32,384,128]{2,1,0:T(8,128)(2,1)}), bf16[32,384,128]{2,1,0:T(8,128)(2,1)}, u32[]{:S(2)}, u32[]{:S(2)}) %all-to-all-start.2) | async-done | bytes 3145760 | tf_op jit(solution)/shard_map/all_to_all | solution.py:485
  212.0 3.5 %unpack.2 = (bf16[128,4096]{1,0:T(8,128)(2,1)}, bf16[128,4096]{1,0:T(8,128)(2,1)}, bf16[128,4096]{1,0:T(8,128)(2,1)}) custom-call(bf16[32,384,128]{2,1,0:T(8,128)(2,1)} %all-to-all-done.2.refs_0_), custom_call_target="tpu_custom_call" | custom-call | bytes 6291456 | tf_op jit(solution)/shard_map/unpack/pallas_call | solution.py:71
  (4 shorter events, 0.1 us)
Async XLA Ops:
  2.8 29.1 %all-to-all-start = ((bf16[32,136,128]{2,1,0:T(8,128)(2,1)}), bf16[32,136,128]{2,1,0:T(8,128)(2,1)S(1)}, u32[]{:S(2)}, u32[]{:S(2)}) async-start(bf16[32,136,128]{2,1,0:T(8,128)(2,1)} %pack.2), calls=%async_computation | async-start | bytes 2228224 | tf_op jit(solution)/shard_map/all_to_all | solution.py:485
  31.8 5.4 %copy-start = (bf16[32,136,128]{2,1,0:T(8,128)(2,1)}, bf16[32,136,128]{2,1,0:T(8,128)(2,1)S(1)}, u32[]{:S(2)}) copy-start(bf16[32,136,128]{2,1,0:T(8,128)(2,1)S(1)} %all-to-all-done.v_ref.info_ref) | copy-start | bytes 3342340
  31.8 57.9 %all-to-all-start.1 = ((bf16[32,512,128]{2,1,0:T(8,128)(2,1)}), bf16[32,512,128]{2,1,0:T(8,128)(2,1)}, u32[]{:S(2)}, u32[]{:S(2)}) async-start(bf16[32,512,128]{2,1,0:T(8,128)(2,1)} %pack.3), calls=%async_computation.1 | async-start | bytes 8388608 | tf_op jit(solution)/shard_map/all_to_all | solution.py:485
  128.6 1.2 collective-permute-start
  130.5 3.9 %collective-permute-start.1 = (f32[64,128]{1,0:T(8,128)S(1)}, f32[64,128]{1,0:T(8,128)S(1)}, u32[]{:S(2)}, u32[]{:S(2)}) collective-permute-start(f32[64,128]{1,0:T(8,128)S(1)} %dynamic-slice_add_fusion), channel_id=1, source_target_pairs={{0,64},{64,0},{32,96},{96,32},{1,65},{65,1},{33,97},{97,33},{2,66}... | collective-permute-start | bytes 98312 | tf_op jit(solution)/shard_map/ppermute | solution.py:506
  166.6 45.5 %all-to-all-start.2 = ((bf16[32,384,128]{2,1,0:T(8,128)(2,1)}), bf16[32,384,128]{2,1,0:T(8,128)(2,1)}, u32[]{:S(2)}, u32[]{:S(2)}) async-start(bf16[32,384,128]{2,1,0:T(8,128)(2,1)} %get-tuple-element.24), calls=%async_computation.2 | async-start | bytes 6291456 | tf_op jit(solution)/shard_map/all_to_all | solution.py:485
  172.6 2.0 collective-permute-start.2
